TPU v7x, 256 devices: a whole 4x4x8 slice. The times are simulated.
256 devices in a mesh: win: 16 (over x_hi, y, core), blk: 16 (over x_lo, z).
Axes of the slice: x: 4 (x_hi: 2, x_lo: 2; x = x_hi * 2 + x_lo), y: 4, z: 8, core: 2. Of those that a mesh axis runs over, the one named last changes fastest.
Arguments:
- sample: float32 [512, 16, 8, 128], P(('win', 'blk')), parts along dimension 0, may hold values from -6 to 6
- fresh_noise: float32 [512, 16, 8, 128], P(('win', 'blk')), parts along dimension 0, may hold values from -6 to 6
- proxy_month: int32 [65536], P('win'), parts along dimension 0, may hold values from 0 to 31, as said below
- proxy_cell: int32 [65536], P('win'), parts along dimension 0, may hold values from 0 to 2047, as said below
- proxy_var: int32 [65536], P('win'), parts along dimension 0, may hold values from 0 to 7
- observed: float32 [65536], P('win'), parts along dimension 0, may hold values from -8 to 8
- proxy_weight: float32 [65536], P('win'), parts along dimension 0, may hold values from 0.25 to 4
- lift_weight: bfloat16 [64, 8], replicated, may hold values from -2 to 2
- month_kernels: bfloat16 [2, 3, 64, 64], replicated, may hold values from -0.4375 to 0.4375
- grid_kernels: bfloat16 [2, 3, 3, 64, 64], replicated, may hold values from -0.25 to 0.25
- read_weight: bfloat16 [8, 64], replicated, may hold values from -0.75 to 0.75
Outputs:
- updated: float32 [512, 16, 8, 128], P(('win', 'blk')), parts along dimension 0
There are 16 independent parts, one for each index of `win`. A program takes and returns all parts, laid end to end along the dimension named above; an argument that names none is the same for every part. Nothing has to cross between parts.
Inputs may be any that keep to these rules, and one draw needn't show every extreme that they name: `proxy_month`: several observations may fall on the same cell, month and variable. `proxy_cell`: A cell is its latitude row times 128 plus its longitude cell.
All inputs are finite; a program needn't handle non-finite values.
Results may differ from a plain program's by a relative error of at most 0.0035.
Values may be sent and summed in bfloat16 or wider, within the bound.
A program may use at most 64 MiB of HBM per device.

v0:
```python
import jax
import jax.numpy as jnp
from jax import lax
from jax.sharding import PartitionSpec as P

tweedie_gain = 0.5
step_size = 0.25
guide_gain = 4.0
noise_gain = 0.5**0.5


def month_conv(source, kernels, dilation):
    months = source.shape[0]
    padded = jnp.pad(source, ((dilation, dilation), (0, 0), (0, 0), (0, 0)))
    summed = jnp.einsum(
        "dc,tlco->tldo", kernels[0], padded[0:months], preferred_element_type=jnp.float32
    )
    for offset in range(1, 3):
        sliced = padded[offset * dilation : offset * dilation + months]
        summed = summed + jnp.einsum(
            "dc,tlco->tldo", kernels[offset], sliced, preferred_element_type=jnp.float32
        )
    return summed


def grid_conv(source, kernels):
    lat_rows = source.shape[1]
    lon_cells = source.shape[3]
    padded = jnp.pad(source, ((0, 0), (1, 1), (0, 0), (1, 1)))
    summed = jnp.zeros(source.shape, jnp.float32)
    for lat_shift in range(3):
        for lon_shift in range(3):
            sliced = padded[
                :, lat_shift : lat_shift + lat_rows, :, lon_shift : lon_shift + lon_cells
            ]
            summed = summed + jnp.einsum(
                "dc,tlco->tldo",
                kernels[lat_shift, lon_shift],
                sliced,
                preferred_element_type=jnp.float32,
            )
    return summed


def flip_months(kernels):
    return jnp.swapaxes(kernels[::-1], 1, 2)


def flip_grid(kernels):
    return jnp.swapaxes(kernels[::-1, ::-1], 2, 3)


def gelu_back(inner, cotangent):
    return jax.vjp(jax.nn.gelu, inner)[1](cotangent)[0]


def next_hidden(hidden, inner):
    return (hidden.astype(jnp.float32) + jax.nn.gelu(inner)).astype(jnp.bfloat16)


def month_layer(hidden, kernels, dilation):
    inner = month_conv(hidden, kernels, dilation)
    return (inner, next_hidden(hidden, inner))


def grid_layer(hidden, kernels):
    inner = grid_conv(hidden, kernels)
    return (inner, next_hidden(hidden, inner))


def month_back(adjoint, inner, kernels, dilation):
    scaled = gelu_back(inner, adjoint.astype(jnp.float32)).astype(jnp.bfloat16)
    spread = month_conv(scaled, flip_months(kernels), dilation)
    return (adjoint.astype(jnp.float32) + spread).astype(jnp.bfloat16)


def grid_back(adjoint, inner, kernels):
    scaled = gelu_back(inner, adjoint.astype(jnp.float32)).astype(jnp.bfloat16)
    spread = grid_conv(scaled, flip_grid(kernels))
    return (adjoint.astype(jnp.float32) + spread).astype(jnp.bfloat16)


def lift_input(lift_weight, states):
    return jnp.einsum(
        "cv,tlvo->tlco", lift_weight.astype(jnp.float32), states, precision=lax.Precision.HIGHEST
    ).astype(jnp.bfloat16)


def lift_transpose(lift_weight, adjoint_zero):
    return jnp.einsum(
        "cv,tlco->tlvo", lift_weight, adjoint_zero, preferred_element_type=jnp.float32
    )


def shards(
    sample,
    fresh_noise,
    proxy_month,
    proxy_cell,
    proxy_var,
    observed,
    proxy_weight,
    lift_weight,
    month_kernels,
    grid_kernels,
    read_weight,
):
    months_dev = sample.shape[0]
    lat_rows = sample.shape[1]
    var_count = sample.shape[2]
    lon_cells = sample.shape[3]
    block_index = lax.axis_index("blk")
    rows_sample = lax.all_to_all(sample, "blk", split_axis=1, concat_axis=0, tiled=True)
    hidden_zero = lift_input(lift_weight, rows_sample)
    inner_one, hidden_one = month_layer(hidden_zero, month_kernels[0], 1)
    inner_two, hidden_two = month_layer(hidden_one, month_kernels[1], 2)
    grid_source = lax.all_to_all(hidden_two, "blk", split_axis=0, concat_axis=1, tiled=True)
    inner_three, hidden_three = grid_layer(grid_source, grid_kernels[0])
    inner_four, hidden_four = grid_layer(hidden_three, grid_kernels[1])
    score_local = jnp.einsum(
        "vc,tlco->tlvo", read_weight, hidden_four, preferred_element_type=jnp.float32
    )
    denoised = sample + tweedie_gain * score_local
    local_month = proxy_month - block_index * months_dev
    owning = jnp.logical_and(local_month >= 0, local_month < months_dev)
    safe_month = jnp.where(owning, local_month, 0)
    flat_index = (
        (safe_month * lat_rows + proxy_cell // lon_cells) * var_count + proxy_var
    ) * lon_cells + proxy_cell % lon_cells
    misfit = denoised.reshape(-1)[flat_index] - observed
    misfit_terms = jnp.where(owning, proxy_weight * misfit * misfit, 0.0)
    misfit_total = lax.psum(jnp.sum(misfit_terms), "blk")
    misfit_norm = jnp.sqrt(misfit_total / proxy_month.shape[0] + 1e-05)
    forcing = jnp.where(owning, guide_gain * proxy_weight * misfit / misfit_norm, 0.0)
    adjoint_denoised = (
        jnp.zeros((sample.size,), jnp.float32).at[flat_index].add(forcing).reshape(sample.shape)
    )
    adjoint_four = jnp.einsum(
        "vc,tlvo->tlco",
        read_weight.astype(jnp.float32),
        tweedie_gain * adjoint_denoised,
        precision=lax.Precision.HIGHEST,
    ).astype(jnp.bfloat16)
    adjoint_three = grid_back(adjoint_four, inner_four, grid_kernels[1])
    adjoint_two = grid_back(adjoint_three, inner_three, grid_kernels[0])
    band_adjoint = lax.all_to_all(adjoint_two, "blk", split_axis=1, concat_axis=0, tiled=True)
    adjoint_one = month_back(band_adjoint, inner_two, month_kernels[1], 2)
    adjoint_zero = month_back(adjoint_one, inner_one, month_kernels[0], 1)
    rows_back = lift_transpose(lift_weight, adjoint_zero)
    lifted_back = lax.all_to_all(
        rows_back.astype(jnp.bfloat16), "blk", split_axis=0, concat_axis=1, tiled=True
    ).astype(rows_back.dtype)
    gradient = adjoint_denoised + lifted_back
    return sample + step_size * (score_local - gradient) + noise_gain * fresh_noise


def solution(mesh):
    in_specs = (
        P(("win", "blk"), None, None, None),
        P(("win", "blk"), None, None, None),
        P("win"),
        P("win"),
        P("win"),
        P("win"),
        P("win"),
        P(),
        P(),
        P(),
        P(),
    )
    out_specs = P(("win", "blk"), None, None, None)
    return jax.shard_map(shards, mesh=mesh, in_specs=in_specs, out_specs=out_specs, check_vma=False)
```

profile of v0, /device:TPU:16, one launch (start us, length us, event | category | flops | bytes accessed | tf_op | source)
XLA Modules:
  0.0 177.5 jit_solution(17756192294454688354)
XLA Ops:
  0.0 0.9 copy.85
  1.0 17.9 %all_to_all.51 = f32[2,16,8,128]{3,2,0,1:T(8,128)S(1)} all-to-all(f32[2,16,8,128]{3,2,0,1:T(8,128)S(1)} %copy.85), channel_id=1, replica_groups=mesh['win'=16,'blk'=16] {'blk'}, dimensions={1} | all-to-all | bytes 262144 | tf_op jit(solution)/shard_map/all_to_all | solution.py:113
  18.8 1.3 convolution_convert_fusion.1
  22.1 1.2 fusion.82
  23.4 3.7 %all-to-all-start.1 = ((bf16[32,1,64,128]{3,2,1,0:T(8,128)(2,1)}), bf16[32,1,64,128]{3,2,1,0:T(8,128)(2,1)S(1)}, u32[]{:S(2)}, u32[]{:S(2)}) async-start(bf16[32,1,64,128]{3,2,1,0:T(8,128)(2,1)} %fusion.82), calls=%async_computation.1 | async-start | bytes 1048576 | tf_op jit(solution)/shard_map/all_to_all | solution.py:117
  27.1 0.7 reverse_bitcast_fusion.1
  28.5 12.5 %all-to-all-done.1 = bf16[32,1,64,128]{3,2,1,0:T(8,128)(2,1)S(1)} async-done(((bf16[32,1,64,128]{3,2,1,0:T(8,128)(2,1)}), bf16[32,1,64,128]{3,2,1,0:T(8,128)(2,1)S(1)}, u32[]{:S(2)}, u32[]{:S(2)}) %all-to-all-start.1) | async-done | bytes 524320 | tf_op jit(solution)/shard_map/all_to_all | solution.py:117
  43.7 1.6 add_convert_fusion.1
  49.0 1.2 multiply_add_fusion
  50.1 23.1 %gather_fusion = f32[4096]{0:T(1024)S(1)} fusion(f32[32768]{0:T(1024)S(1)} %bitcast.457, s32[4096]{0:T(1024)} %get-tuple-element.5), kind=kCustom, calls=%fused_computation | custom fusion | bytes 49152 | tf_op jit(solution)/shard_map/gather | solution.py:130
  73.9 1.3 fusion.102
  75.2 34.4 %psum.7 = f32[]{:T(128)} all-reduce(f32[]{:T(128)} %fusion.102), channel_id=1, replica_groups=mesh['win'=16,'blk'=16] {'blk'}, use_global_device_ids=true, to_apply=%region_1.2 | all-reduce | flops 1 | bytes 8 | tf_op jit(solution)/shard_map/psum | solution.py:132
  110.3 0.8 divide_select_fusion
  111.1 22.7 %scatter_custom_fusion = f32[32768]{0:T(1024)} fusion(s32[4096]{0:T(1024)} %get-tuple-element.6, f32[4096]{0:T(1024)S(1)} %divide_select_fusion, f32[]{:T(128)} %constant.29.clone.1), kind=kCustom, calls=%fused_computation.195 | custom fusion | flops 4096 | bytes 131584 | tf_op jit(solution)/shard_map/scatter-add | solution.py:136
  133.7 2.2 %fusion.45 = (bf16[2,16,64,128]{3,2,1,0:T(8,128)(2,1)S(1)}, f32[2,16,64,128]{3,2,1,0:T(8,128)S(1)}) fusion(f32[2,16,64,128]{3,2,1,0:T(8,128)S(1)} %fusion.2, bf16[8,64]{1,0:T(8,128)(2,1)S(1)} %copy-done, f32[2,16,8,128]{3,2,1,0:T(8,128)} %bitcast.474), kind=kOutput, calls=%fused_computation.137 | convolution fusion | flops 30965760 | bytes 2753536 | tf_op jit(solution)/shard_map/vc,tlvo->tlco/dot_general | solution.py:138
  138.9 0.9 copy-done.14
  139.8 1.0 fusion.38
  144.3 0.8 copy.106
  145.1 3.6 %all-to-all-start.2 = ((bf16[2,16,64,128]{3,2,0,1:T(8,128)(2,1)}), bf16[2,16,64,128]{3,2,0,1:T(8,128)(2,1)S(1)}, u32[]{:S(2)}, u32[]{:S(2)}) async-start(bf16[2,16,64,128]{3,2,0,1:T(8,128)(2,1)} %copy.106), calls=%async_computation.2 | async-start | bytes 1048576 | tf_op jit(solution)/shard_map/all_to_all | solution.py:146
  149.0 11.2 %all-to-all-done.2 = bf16[2,16,64,128]{3,2,0,1:T(8,128)(2,1)S(1)} async-done(((bf16[2,16,64,128]{3,2,0,1:T(8,128)(2,1)}), bf16[2,16,64,128]{3,2,0,1:T(8,128)(2,1)S(1)}, u32[]{:S(2)}, u32[]{:S(2)}) %all-to-all-start.2) | async-done | bytes 524320 | tf_op jit(solution)/shard_map/all_to_all | solution.py:146
  160.3 0.7 fusion.31
  161.5 0.9 fusion.24
  163.8 12.9 %all_to_all.52 = bf16[32,1,8,128]{3,2,1,0:T(8,128)(2,1)S(1)} all-to-all(bf16[32,1,8,128]{3,2,1,0:T(8,128)(2,1)S(1)} %fusion.17), channel_id=1, replica_groups=mesh['win'=16,'blk'=16] {'blk'}, dimensions={0} | all-to-all | bytes 131072 | tf_op jit(solution)/shard_map/all_to_all | solution.py:150
  176.8 0.7 fusion.91
  (84 shorter events, 18.0 us)
Async XLA Ops:
  0.0 48.4 %copy-start = (bf16[8,64]{1,0:T(8,128)(2,1)S(1)}, bf16[8,64]{1,0:T(8,128)(2,1)}, u32[]{:S(2)}) copy-start(bf16[8,64]{1,0:T(8,128)(2,1)} %param.21) | copy-start | bytes 3076
  0.0 20.1 %copy-start.5 = (bf16[2,3,64,64]{3,2,1,0:T(8,128)(2,1)S(1)}, bf16[2,3,64,64]{3,2,1,0:T(8,128)(2,1)}, u32[]{:S(2)}) copy-start(bf16[2,3,64,64]{3,2,1,0:T(8,128)(2,1)} %param.19) | copy-start | bytes 147460
  23.4 3.7 %copy-start.6 = (bf16[2,3,3,64,64]{4,3,2,1,0:T(8,128)(2,1)S(1)}, bf16[2,3,3,64,64]{4,3,2,1,0:T(8,128)(2,1)}, u32[]{:S(2)}) copy-start(bf16[2,3,3,64,64]{4,3,2,1,0:T(8,128)(2,1)} %param.20) | copy-start | bytes 442372
  23.4 4.5 %copy-start.10 = (s32[4096]{0:T(1024)S(1)}, s32[4096]{0:T(1024)}, u32[]{:S(2)}) copy-start(s32[4096]{0:T(1024)} %param.15) | copy-start | bytes 49156
  23.4 4.5 %copy-start.11 = (s32[4096]{0:T(1024)S(1)}, s32[4096]{0:T(1024)}, u32[]{:S(2)}) copy-start(s32[4096]{0:T(1024)} %param.14) | copy-start | bytes 49156
  23.4 4.5 %copy-start.12 = (s32[4096]{0:T(1024)S(1)}, s32[4096]{0:T(1024)}, u32[]{:S(2)}) copy-start(s32[4096]{0:T(1024)} %param.13) | copy-start | bytes 49156
  23.4 17.6 %all-to-all-start.1 = ((bf16[32,1,64,128]{3,2,1,0:T(8,128)(2,1)}), bf16[32,1,64,128]{3,2,1,0:T(8,128)(2,1)S(1)}, u32[]{:S(2)}, u32[]{:S(2)}) async-start(bf16[32,1,64,128]{3,2,1,0:T(8,128)(2,1)} %fusion.82), calls=%async_computation.1 | async-start | bytes 1048576 | tf_op jit(solution)/shard_map/all_to_all | solution.py:117
  48.0 0.9 copy-start.2
  73.3 0.6 copy-start.7
  133.7 2.2 %copy-start.1 = (bf16[3,3,64,64]{2,3,1,0:T(8,128)(2,1)S(1)}, bf16[3,3,64,64]{2,3,1,0:T(8,128)(2,1)}, u32[]{:S(2)}) copy-start(bf16[3,3,64,64]{2,3,1,0:T(8,128)(2,1)} %reverse_bitcast_fusion.1) | copy-start | bytes 221188
  138.6 1.2 copy-start.14
  145.1 15.0 %all-to-all-start.2 = ((bf16[2,16,64,128]{3,2,0,1:T(8,128)(2,1)}), bf16[2,16,64,128]{3,2,0,1:T(8,128)(2,1)S(1)}, u32[]{:S(2)}, u32[]{:S(2)}) async-start(bf16[2,16,64,128]{3,2,0,1:T(8,128)(2,1)} %copy.106), calls=%async_computation.2 | async-start | bytes 1048576 | tf_op jit(solution)/shard_map/all_to_all | solution.py:146
  162.8 0.7 copy-start.13
  163.4 13.3 %copy-start.3 = (f32[2,16,8,128]{3,2,1,0:T(8,128)S(1)}, f32[2,16,8,128]{3,2,1,0:T(8,128)}, u32[]{:S(2)}) copy-start(f32[2,16,8,128]{3,2,1,0:T(8,128)} %param.11) | copy-start | bytes 393220
  163.4 13.3 %copy-start.4 = (f32[32768]{0:T(1024)S(1)}, f32[32768]{0:T(1024)}, u32[]{:S(2)}) copy-start(f32[32768]{0:T(1024)} %scatter_custom_fusion) | copy-start | bytes 393220
  163.4 13.3 %copy-start.8 = (f32[2,16,8,128]{3,2,1,0:T(8,128)S(1)}, f32[2,16,8,128]{3,2,1,0:T(8,128)}, u32[]{:S(2)}) copy-start(f32[2,16,8,128]{3,2,1,0:T(8,128)} %param.12) | copy-start | bytes 393220
  163.4 13.3 %copy-start.9 = (f32[2,16,8,128]{3,2,1,0:T(8,128)S(1)}, f32[2,16,8,128]{3,2,1,0:T(8,128)}, u32[]{:S(2)}) copy-start(f32[2,16,8,128]{3,2,1,0:T(8,128)} %get-tuple-element.17) | copy-start | bytes 393220
where the time goes:
time: 178 us; the launch traced here: 177 us
  blocking collectives  65.2 us (37%)
  local copies, waits for them, and re-layouts  28.3 us (16%)
  other arithmetic  28.1 us (16%)
  waiting for transfers between devices  23.7 us (13%)
  matrix products  23.6 us (13%)
  starting transfers between devices  7.29 us (4%)
    psum x1, blocking collectives, shards(): misfit_total = lax.psum(jnp.sum(misfit_terms), 'blk')  34.4 us
    gather x1, local copies, waits for them, and re-layouts, shards(): misfit = denoised.reshape(-1)[flat_index] - observed  23.1 us
    scatter-add x1, other arithmetic, shards(): jnp.zeros((sample.size,), jnp.float32).at[flat_index].add(forcing)  22.7 us
    all_to_all x1, blocking collectives, shards(): lax.all_to_all(sample, 'blk', split_axis=1, concat_axis=0, tiled=True)  17.9 us
    dot_general x36, matrix products, grid_conv(): jnp.einsum('dc,tlco->tldo', kernels[lat_shift, lon_shift], sliced, prefer...  14.6 us
    all_to_all x1, blocking collectives, shards(): lax.all_to_all(rows_back.astype(jnp.bfloat16), 'blk', split_axis=0, conca...  12.9 us
    all_to_all x1, waiting for transfers between devices, shards(): lax.all_to_all(hidden_two, 'blk', split_axis=0, concat_axis=1, tiled=True)  12.5 us
    all_to_all x1, waiting for transfers between devices, shards(): lax.all_to_all(adjoint_two, 'blk', split_axis=1, concat_axis=0, tiled=True)  11.2 us
  transfers between devices with their start and end apart: 2, of which 2 were waited for; matrix products, arithmetic and copies ran while one was open for 1% of the time, Pallas kernels for 0%

commit v1 on v0

v1 whole, which is shorter than its diff:
```python
import functools

import jax
import jax.numpy as jnp
from jax import lax
from jax.experimental import pallas as pl
from jax.experimental.pallas import tpu as pltpu
from jax.sharding import PartitionSpec as P

tweedie_gain = 0.5
step_size = 0.25
guide_gain = 4.0
noise_gain = 0.5**0.5

f32 = jnp.float32
bf16 = jnp.bfloat16
MESH = pl.DeviceIdType.MESH

gelu_c = 0.7978845608028654
gelu_ca = gelu_c * 0.044715


def gelu_parts(x):
    x2 = x * x
    u = x * (gelu_c + gelu_ca * x2)
    h = 0.5 * jnp.tanh(u) + 0.5
    g = x * h
    dg = h + (g - g * h) * (2.0 * gelu_c + 6.0 * gelu_ca * x2)
    return g, dg


def dot(a, b):
    return jnp.dot(a, b, preferred_element_type=f32)


def dot_nt(a, b):
    return lax.dot_general(a, b, (((1,), (1,)), ((), ())), preferred_element_type=f32)


def lanes(*parts):
    return jnp.concatenate(parts, axis=1)


def rows(*parts):
    return jnp.concatenate(parts, axis=0)


def lon_sum(out, first, last):
    halves = []
    for m in range(2):
        cols = slice(128 * m, 128 * (m + 1))
        left = pltpu.roll(out[0:128, cols], 1, 1)
        right = pltpu.roll(out[256:384, cols], 127, 1)
        total = out[128:256, cols] + jnp.where(first, 0.0, left) + jnp.where(last, 0.0, right)
        halves.append(total)
    return lanes(*halves)


def grid_weights(block):
    zero = jnp.zeros((64, 64), f32)
    out = []
    for b in range(3):
        k0, k1, k2 = block(0, b), block(1, b), block(2, b)
        out.append(lanes(k0, k1, k2, zero))
        out.append(lanes(zero, k0, k1, k2))
    return rows(*out).astype(bf16)


def kernel(
    blk,
    sample_ref, noise_ref, month_ref, cell_ref, var_ref, obs_ref, pw_ref,
    lift_ref, mk_ref, gk_ref, read_ref,
    out_ref,
    send_pair, send_lo, send_hi, halo_l, halo_r, halo_ll, halo_rr,
    wf1, wf2, wf3, wf4, wb4, wb3, wb2, wb1, wread, wreadt,
    field,
    g1, g2, g3, g4, h2s, h3s, s4s, s3s, a4, a3,
    base, grad,
    gs_l, gs_r, gs_ll, gs_rr, gr_l, gr_r, gr_ll, gr_rr,
    psend, pbuf,
    hs_sem, hr_sem, gs_sem, gr_sem, ps_sem, pr_sem,
):
    me = lax.axis_index("blk")

    def peer(k):
        return lax.rem(me + k + blk, blk)

    def remote(src, dst, ssem, rsem, k):
        return pltpu.make_async_remote_copy(
            src_ref=src, dst_ref=dst, send_sem=ssem, recv_sem=rsem,
            device_id={"blk": peer(k)}, device_id_type=MESH,
        )

    barrier = pltpu.get_barrier_semaphore()
    for k in range(1, blk):
        pl.semaphore_signal(barrier, inc=1, device_id={"blk": peer(k)}, device_id_type=MESH)

    for l in range(16):
        send_pair[l] = rows(sample_ref[0, l], sample_ref[1, l]).astype(bf16)
    for q in range(8):
        send_lo[q] = rows(sample_ref[0, 2 * q], sample_ref[0, 2 * q + 1]).astype(bf16)
        send_hi[q] = rows(sample_ref[1, 2 * q], sample_ref[1, 2 * q + 1]).astype(bf16)

    pl.semaphore_wait(barrier, blk - 1)
    halo = [
        remote(send_pair, halo_l, hs_sem.at[0], hr_sem.at[0], 1),
        remote(send_pair, halo_r, hs_sem.at[1], hr_sem.at[1], -1),
        remote(send_hi, halo_ll, hs_sem.at[2], hr_sem.at[2], 2),
        remote(send_lo, halo_rr, hs_sem.at[3], hr_sem.at[3], -2),
    ]
    for copy in halo:
        copy.start()

    has_l = jnp.where(me > 0, 1.0, 0.0).astype(f32)
    has_ll = jnp.where(me > 1, 1.0, 0.0).astype(f32)
    has_r = jnp.where(me < blk - 1, 1.0, 0.0).astype(f32)
    has_rr = jnp.where(me < blk - 2, 1.0, 0.0).astype(f32)

    lift = lift_ref[...]
    pick = (lax.broadcasted_iota(jnp.int32, (8, 64), 1) % 8
            == lax.broadcasted_iota(jnp.int32, (8, 64), 0))
    tiled = dot(lift, jnp.where(pick, 1.0, 0.0).astype(bf16))
    col_month = lax.broadcasted_iota(jnp.int32, (64, 64), 1) // 8
    placed = [jnp.where(col_month == i, tiled, 0.0) for i in range(8)]
    placed_b = [x.astype(bf16) for x in placed]
    inner_rows = []
    for j in range(6):
        acc = dot(mk_ref[0, 0], placed_b[j])
        acc = acc + dot(mk_ref[0, 1], placed_b[j + 1])
        acc = acc + dot(mk_ref[0, 2], placed_b[j + 2])
        inner_rows.append(acc)
    both = rows(*inner_rows, *placed[1:7])
    both_hi = both.astype(bf16).astype(f32)
    both_lo = both - both_hi
    wf1[...] = lanes(both_hi, both_lo, both_hi, jnp.zeros_like(both)).astype(bf16)
    flipped_hi = jnp.transpose(both_hi)
    flipped_lo = jnp.transpose(both_lo)
    wb1[...] = rows(flipped_hi, flipped_lo).astype(bf16)

    def mk(k):
        return mk_ref[1, k].astype(f32)

    wf2[...] = lanes(mk(0) * has_l, mk(1), mk(2) * has_r).astype(bf16)
    wb2[...] = rows(
        jnp.transpose(mk(0)) * has_l, jnp.transpose(mk(1)), jnp.transpose(mk(2)) * has_r
    ).astype(bf16)
    wf3[...] = grid_weights(lambda a, b: gk_ref[0, a, b].astype(f32))
    wf4[...] = grid_weights(lambda a, b: gk_ref[1, a, b].astype(f32))
    wb3[...] = grid_weights(lambda a, b: jnp.transpose(gk_ref[0, 2 - a, 2 - b].astype(f32)))
    wb4[...] = grid_weights(lambda a, b: jnp.transpose(gk_ref[1, 2 - a, 2 - b].astype(f32)))
    read = read_ref[...].astype(f32)
    zero_read = jnp.zeros((8, 64), f32)
    wide = rows(lanes(read, zero_read), lanes(zero_read, read))
    wread[...] = wide.astype(bf16)
    tall = jnp.transpose(wide)
    wreadt[...] = lanes(tall, tall).astype(bf16)

    local = month_ref[...] - 2 * me
    owned = jnp.logical_and(local >= 0, local < 2)
    cell = cell_ref[...]
    row_of = jnp.where(owned, (local * 16 + lax.shift_right_logical(cell, 7)) * 8 + var_ref[...], -1)
    lon_of = jnp.bitwise_and(cell, 127)
    weight = pw_ref[...]
    weighted = weight * obs_ref[...]
    w_hi = weight.astype(bf16).astype(f32)
    w_lo = (weight - w_hi).astype(bf16).astype(f32)
    b_hi = weighted.astype(bf16).astype(f32)
    b_lo = (weighted - b_hi).astype(bf16).astype(f32)
    b_sum = b_hi + b_lo
    spread_terms = jnp.where(owned, b_sum * b_sum / (w_hi + w_lo), 0.0)
    within = (spread_terms[0:8] + spread_terms[8:16]) + (spread_terms[16:24] + spread_terms[24:32])
    row_iota = lax.broadcasted_iota(jnp.int32, (256, 128), 0)
    lon_iota = lax.broadcasted_iota(jnp.int32, (128, 128), 0)
    for c in range(4):
        lhs, rhs = [], []
        for r in range(8 * c, 8 * c + 8):
            lhs.append(jnp.where(row_iota == row_of[r:r + 1], 1.0, 0.0).astype(bf16))
            at = lon_iota == lon_of[r:r + 1]
            rhs.append(rows(*[
                jnp.where(at, x[r:r + 1], 0.0).astype(bf16) for x in (w_hi, w_lo, b_hi, b_lo)
            ]))
        part = dot_nt(lanes(*lhs), lanes(*rhs))
        if c == 0:
            field[...] = part
        else:
            field[...] += part
    w_field = field[:, 0:128] + field[:, 128:256]
    b_field = field[:, 256:384] + field[:, 384:512]
    mean = jnp.where(w_field > 0.0, b_field / jnp.where(w_field > 0.0, w_field, 1.0), 0.0)
    field[:, 0:128] = w_field
    field[:, 128:256] = mean
    taken = b_field * mean
    for r in range(32):
        within = within - taken[8 * r:8 * r + 8]

    zero_row = jnp.zeros((64, 256), bf16)
    for ref in (h2s, h3s, s4s, s3s):
        ref[0] = zero_row
        ref[17] = zero_row

    lane = lax.broadcasted_iota(jnp.int32, (128, 128), 1)
    first, last = lane == 0, lane == 127

    for copy in halo:
        copy.wait_recv()

    def month_step(q, carry):
        highs, lows = [], []
        for i in range(2):
            l = 2 * q + i
            prev = halo_l[l].astype(f32) * has_l
            nxt = halo_r[l].astype(f32) * has_r
            prev2 = halo_ll[q].astype(f32)[8 * i:8 * i + 8] * has_ll
            nxt2 = halo_rr[q].astype(f32)[8 * i:8 * i + 8] * has_rr
            own = rows(sample_ref[0, l], sample_ref[1, l])
            own_hi = own.astype(bf16).astype(f32)
            highs.append(rows(prev2, prev, own_hi, nxt, nxt2))
            z = jnp.zeros((24, 128), f32)
            lows.append(rows(z, own - own_hi, z))
        high = lanes(*highs)
        src = rows(high, high, lanes(*lows), jnp.zeros((64, 256), f32)).astype(bf16)
        out = dot(wf1[...], src)
        gel, der = gelu_parts(out[0:384])
        g1[q] = der
        hidden = out[384:768] + gel
        hidden_b = hidden.astype(bf16)
        for m in range(2):
            src2 = rows(*[hidden_b[64 * j:64 * j + 64] for j in (m, m + 2, m + 4)])
            gel2, der2 = gelu_parts(dot(wf2[...], src2))
            g2[q, m] = der2
            nxt_h = (hidden[64 * (m + 2):64 * (m + 3)] + gel2).astype(bf16)
            for i in range(2):
                h2s[2 * q + i + 1, :, 128 * m:128 * m + 128] = nxt_h[:, 128 * i:128 * i + 128]
        return carry

    lax.fori_loop(0, 8, month_step, 0)

    def window(ref, q):
        return ref[pl.ds(2 * q, 4)].reshape(256, 256)

    def pair(ref, q, at):
        return ref[pl.ds(2 * q + at, 2)].reshape(128, 256)

    def grid_step(q, carry):
        inner = lon_sum(dot(wf3[...], window(h2s, q)), first, last)
        gel, der = gelu_parts(inner)
        g3[q] = der
        h3s[pl.ds(2 * q + 1, 2)] = (pair(h2s, q, 1).astype(f32) + gel).astype(bf16).reshape(2, 64, 256)
        return carry

    lax.fori_loop(0, 8, grid_step, 0)

    def top_step(q, total):
        inner = lon_sum(dot(wf4[...], window(h3s, q)), first, last)
        gel, der = gelu_parts(inner)
        hidden = (pair(h3s, q, 1).astype(f32) + gel).astype(bf16)
        score = dot(wread[...], hidden)
        forces = []
        for i in range(2):
            l = 2 * q + i
            line = []
            for m in range(2):
                sc = score[8 * i:8 * i + 8, 128 * m:128 * m + 128]
                sm = sample_ref[m, l]
                at = pl.ds((m * 16 + l) * 8, 8)
                w = field[at, 0:128]
                delta = sm + tweedie_gain * sc - field[at, 128:256]
                pull = w * delta
                total = total + pull * delta
                force = guide_gain * pull
                base[m, l] = sm + step_size * sc + noise_gain * noise_ref[m, l]
                grad[m, l] = force
                line.append(tweedie_gain * force)
            forces.append(lanes(*line))
        force = rows(*forces)
        force_hi = force.astype(bf16).astype(f32)
        src = rows(force_hi, force - force_hi).astype(bf16)
        adj = dot(wreadt[...], src)
        a4[q] = adj
        s4s[pl.ds(2 * q + 1, 2)] = (adj * der).astype(bf16).reshape(2, 64, 256)
        return total

    total = lax.fori_loop(0, 8, top_step, within)

    psend[...] = total
    sums = [
        remote(psend, pbuf.at[k], ps_sem.at[k], pr_sem.at[k], k) for k in range(1, blk)
    ]
    for copy in sums:
        copy.start()

    def back_step(q, carry):
        adj = a4[q] + lon_sum(dot(wb4[...], window(s4s, q)), first, last)
        a3[q] = adj
        s3s[pl.ds(2 * q + 1, 2)] = (adj * g3[q]).astype(bf16).reshape(2, 64, 256)
        return carry

    lax.fori_loop(0, 8, back_step, 0)

    def low_step(q, carry):
        adj2 = a3[q] + lon_sum(dot(wb3[...], window(s3s, q)), first, last)
        own, pushed = [], []
        for m in range(2):
            cols = slice(128 * m, 128 * m + 128)
            adj = lanes(adj2[0:64, cols], adj2[64:128, cols])
            own.append(adj)
            scaled = (adj * g2[q, m]).astype(bf16)
            pushed.append(dot(wb2[...], scaled))
        adj1 = rows(
            pushed[0][0:64], pushed[1][0:64],
            own[0] + pushed[0][64:128], own[1] + pushed[1][64:128],
            pushed[0][128:192], pushed[1][128:192],
        )
        scaled1 = (adj1 * g1[q]).astype(bf16)
        both = dot(wb1[...], rows(scaled1, adj1.astype(bf16)))
        part = both[0:64] + both[64:128]
        for i in range(2):
            l = 2 * q + i
            cols = slice(128 * i, 128 * i + 128)
            gs_l[l] = part[8:24, cols].astype(bf16)
            gs_r[l] = part[40:56, cols].astype(bf16)
            for m in range(2):
                grad[m, l] += part[24 + 8 * m:32 + 8 * m, cols]
        gs_ll[q] = rows(part[0:8, 0:128], part[0:8, 128:256]).astype(bf16)
        gs_rr[q] = rows(part[56:64, 0:128], part[56:64, 128:256]).astype(bf16)
        return carry

    lax.fori_loop(0, 8, low_step, 0)
    back = [
        remote(gs_r, gr_l, gs_sem.at[0], gr_sem.at[0], 1),
        remote(gs_l, gr_r, gs_sem.at[1], gr_sem.at[1], -1),
        remote(gs_rr, gr_ll, gs_sem.at[2], gr_sem.at[2], 2),
        remote(gs_ll, gr_rr, gs_sem.at[3], gr_sem.at[3], -2),
    ]
    for copy in back:
        copy.start()

    for copy in sums:
        copy.wait_recv()
    tile = psend[...]
    for k in range(1, blk):
        tile = tile + pbuf[k]
    full = jnp.sum(jnp.sum(tile, axis=1, keepdims=True), axis=0, keepdims=True)
    norm = jnp.sqrt(full / 4096.0 + 1e-05)
    scale = jnp.broadcast_to(step_size / norm, (8, 128))

    for copy in back:
        copy.wait_recv()
    for q in range(8):
        far_l = gr_ll[q].astype(f32) * has_ll
        far_r = gr_rr[q].astype(f32) * has_rr
        for i in range(2):
            l = 2 * q + i
            near = gr_l[l].astype(f32) * has_l + gr_r[l].astype(f32) * has_r
            far = (far_l[8 * i:8 * i + 8], far_r[8 * i:8 * i + 8])
            for m in range(2):
                g = grad[m, l] + near[8 * m:8 * m + 8] + far[m]
                out_ref[m, l] = base[m, l] - scale * g

    for copy in halo + sums + back:
        copy.wait_send()


def shards(
    blk,
    sample, fresh_noise, proxy_month, proxy_cell, proxy_var, observed, proxy_weight,
    lift_weight, month_kernels, grid_kernels, read_weight,
):
    def grid(x):
        return x.reshape(32, 128)

    vmem = pltpu.VMEM
    dma = pltpu.SemaphoreType.DMA
    scratch = [
        vmem((16, 16, 128), bf16), vmem((8, 16, 128), bf16), vmem((8, 16, 128), bf16),
        vmem((16, 16, 128), bf16), vmem((16, 16, 128), bf16),
        vmem((8, 16, 128), bf16), vmem((8, 16, 128), bf16),
        vmem((768, 256), bf16), vmem((64, 192), bf16),
        vmem((384, 256), bf16), vmem((384, 256), bf16), vmem((384, 256), bf16), vmem((384, 256), bf16),
        vmem((192, 64), bf16), vmem((128, 768), bf16),
        vmem((16, 128), bf16), vmem((128, 32), bf16),
        vmem((256, 512), f32),
        vmem((8, 384, 256), f32), vmem((8, 2, 64, 256), f32),
        vmem((8, 128, 256), f32), vmem((8, 128, 256), f32),
        vmem((18, 64, 256), bf16), vmem((18, 64, 256), bf16),
        vmem((18, 64, 256), bf16), vmem((18, 64, 256), bf16),
        vmem((8, 128, 256), f32), vmem((8, 128, 256), f32),
        vmem((2, 16, 8, 128), f32), vmem((2, 16, 8, 128), f32),
        vmem((16, 16, 128), bf16), vmem((16, 16, 128), bf16),
        vmem((8, 16, 128), bf16), vmem((8, 16, 128), bf16),
        vmem((16, 16, 128), bf16), vmem((16, 16, 128), bf16),
        vmem((8, 16, 128), bf16), vmem((8, 16, 128), bf16),
        vmem((8, 128), f32), vmem((blk, 8, 128), f32),
        dma((4,)), dma((4,)), dma((4,)), dma((4,)), dma((blk,)), dma((blk,)),
    ]
    return pl.pallas_call(
        functools.partial(kernel, blk),
        out_shape=jax.ShapeDtypeStruct(sample.shape, f32),
        in_specs=[pl.BlockSpec(memory_space=pltpu.VMEM)] * 11,
        out_specs=pl.BlockSpec(memory_space=pltpu.VMEM),
        scratch_shapes=scratch,
        compiler_params=pltpu.CompilerParams(collective_id=0, has_side_effects=True),
        name="guided_step",
    )(
        sample, fresh_noise, grid(proxy_month), grid(proxy_cell), grid(proxy_var),
        grid(observed), grid(proxy_weight), lift_weight, month_kernels, grid_kernels, read_weight,
    )


def solution(mesh):
    in_specs = (
        P(("win", "blk"), None, None, None),
        P(("win", "blk"), None, None, None),
        P("win"),
        P("win"),
        P("win"),
        P("win"),
        P("win"),
        P(),
        P(),
        P(),
        P(),
    )
    out_specs = P(("win", "blk"), None, None, None)
    return jax.shard_map(
        functools.partial(shards, mesh.shape["blk"]),
        mesh=mesh, in_specs=in_specs, out_specs=out_specs, check_vma=False,
    )
```

time: 178 us -> 45 us (0.25)
  blocking collectives: 65.2 us -> 0 us
  Pallas kernels: 0 us -> 41.9 us
  other arithmetic: 28.1 us -> 0 us
  local copies, waits for them, and re-layouts: 28.3 us -> 2.95 us
  waiting for transfers between devices: 23.7 us -> 0 us
  matrix products: 23.6 us -> 0 us
  starting transfers between devices: 7.29 us -> 0 us
    pallas_call x0 -> x1, Pallas kernels: none -> 41.9 us  [shards(): pl.pallas_call(functools.partial(kernel, blk), out_shape=jax.ShapeDtypeSt...]
    psum x1 -> x0, blocking collectives: 34.4 us -> none  [shards(): misfit_total = lax.psum(jnp.sum(misfit_terms), 'blk')]
    all_to_all x2 -> x0, blocking collectives: 30.8 us -> none  [the longest x1 17.9 us: shards(): lax.all_to_all(sample, 'blk', split_axis=1, concat_axis=0, tiled=True)]
    all_to_all x2 -> x0, waiting for transfers between devices: 23.7 us -> none  [the longest x1 12.5 us: shards(): lax.all_to_all(hidden_two, 'blk', split_axis=0, concat_axis=1, tiled=True)]
    dot_general x51 -> x0, matrix products: 23.6 us -> none  [the longest x36 14.6 us: grid_conv(): jnp.einsum('dc,tlco->tldo', kernels[lat_shift, lon_shift], sliced, prefer...]
    gather x1 -> x0, local copies, waits for them, and re-layouts: 23.1 us -> none  [shards(): misfit = denoised.reshape(-1)[flat_index] - observed]
    scatter-add x1 -> x0, other arithmetic: 22.7 us -> none  [shards(): jnp.zeros((sample.size,), jnp.float32).at[flat_index].add(forcing)]
    all_to_all x2 -> x0, starting transfers between devices: 7.29 us -> none  [the longest x1 3.71 us: shards(): lax.all_to_all(hidden_two, 'blk', split_axis=0, concat_axis=1, tiled=True)]
  transfers between devices with their start and end apart: 2 -> 0, of which waited for: 2 -> 0; matrix products, arithmetic and copies ran while one was open for 1% -> 0% of each run, Pallas kernels for 0% -> 0%
where the time goes in v1:
time: 45 us; the launch traced here: 44.8 us
  Pallas kernels  41.9 us (93%)
  local copies, waits for them, and re-layouts  2.95 us (7%)
    pallas_call x1, Pallas kernels, shards(): pl.pallas_call(functools.partial(kernel, blk), out_shape=jax.ShapeDtypeSt...  41.9 us
    unnamed x4, local copies, waits for them, and re-layouts  2.95 us

profile of v1, /device:TPU:16, one launch (start us, length us, event | category | flops | bytes accessed | tf_op | source)
XLA Modules:
  0.0 44.8 jit_solution(4228344506540460374)
XLA Ops:
  0.0 0.0 copy-start
  0.0 0.7 %copy-done = bf16[64,8]{0,1:T(8,128)(2,1)S(1)} copy-done((bf16[64,8]{0,1:T(8,128)(2,1)S(1)}, bf16[64,8]{0,1:T(8,128)(2,1)}, u32[]{:S(2)}) %copy-start) | copy-done | bytes 1048
  0.7 0.7 %copy.12.lift_ref = bf16[64,8]{1,0:T(8,128)(2,1)} copy(bf16[64,8]{0,1:T(8,128)(2,1)S(1)} %copy-done) | data formatting | bytes 2048 | tf_op args[7]
  1.4 41.9 %guided_step.1 = f32[2,16,8,128]{3,2,1,0:T(8,128)} custom-call(f32[2,16,8,128]{3,2,1,0:T(8,128)} %sample_ref.1, f32[2,16,8,128]{3,2,1,0:T(8,128)} %noise_ref.1, s32[32,128]{1,0:T(8,128)} %bitcast.5, s32[32,128]{1,0:T(8,128)} %bitcast.6, s32[32,128]{1,0:T(8,128)} %bitcast.7, f32[32,128]{1,0:T(8,128)} %bitcast.8, f32[32,128]{1,0:T(8,128)} %bitcast.9, ...), custom_call_target="tpu_custom_call" | custom-call | tf_op jit(solution)/shard_map/guided_step/pallas_call | solution.py:396
  43.3 1.6 %copy.14 = f32[2,16,8,128]{3,2,1,0:T(8,128)} copy(f32[2,16,8,128]{3,2,1,0:T(8,128)} %guided_step.1) | data formatting | bytes 262144
Async XLA Ops:
  0.0 0.7 %copy-start = (bf16[64,8]{0,1:T(8,128)(2,1)S(1)}, bf16[64,8]{0,1:T(8,128)(2,1)}, u32[]{:S(2)}) copy-start(bf16[64,8]{0,1:T(8,128)(2,1)} %param.18) | copy-start | bytes 3076

commit v2 on v1

--- a/solution.py
+++ b/solution.py
@@ -68,9 +68,11 @@
 
 def kernel(
     blk,
+    sample_in, noise_in, month_in, cell_in, var_in, obs_in, pw_in,
+    lift_in, mk_in, gk_in, read_in,
+    out_ref,
     sample_ref, noise_ref, month_ref, cell_ref, var_ref, obs_ref, pw_ref,
     lift_ref, mk_ref, gk_ref, read_ref,
-    out_ref,
     send_pair, send_lo, send_hi, halo_l, halo_r, halo_ll, halo_rr,
     wf1, wf2, wf3, wf4, wb4, wb3, wb2, wb1, wread, wreadt,
     field,
@@ -78,7 +80,7 @@
     base, grad,
     gs_l, gs_r, gs_ll, gs_rr, gr_l, gr_r, gr_ll, gr_rr,
     psend, pbuf,
-    hs_sem, hr_sem, gs_sem, gr_sem, ps_sem, pr_sem,
+    hs_sem, hr_sem, gs_sem, gr_sem, ps_sem, pr_sem, in_sem, near_sem, far_sem,
 ):
     me = lax.axis_index("blk")
 
@@ -91,9 +93,24 @@
             device_id={"blk": peer(k)}, device_id_type=MESH,
         )
 
+    def signal(sem, k):
+        pl.semaphore_signal(sem, inc=1, device_id={"blk": peer(k)}, device_id_type=MESH)
+
     barrier = pltpu.get_barrier_semaphore()
-    for k in range(1, blk):
-        pl.semaphore_signal(barrier, inc=1, device_id={"blk": peer(k)}, device_id_type=MESH)
+    for k in (2, -2, 1, -1):
+        signal(barrier, k)
+
+    loads = [
+        pltpu.make_async_copy(src, dst, in_sem.at[n])
+        for n, (src, dst) in enumerate((
+            (sample_in, sample_ref), (mk_in, mk_ref), (lift_in, lift_ref), (gk_in, gk_ref),
+            (read_in, read_ref), (month_in, month_ref), (cell_in, cell_ref), (var_in, var_ref),
+            (obs_in, obs_ref), (pw_in, pw_ref), (noise_in, noise_ref),
+        ))
+    ]
+    for copy in loads:
+        copy.start()
+    loads[0].wait()
 
     for l in range(16):
         send_pair[l] = rows(sample_ref[0, l], sample_ref[1, l]).astype(bf16)
@@ -101,15 +118,28 @@
         send_lo[q] = rows(sample_ref[0, 2 * q], sample_ref[0, 2 * q + 1]).astype(bf16)
         send_hi[q] = rows(sample_ref[1, 2 * q], sample_ref[1, 2 * q + 1]).astype(bf16)
 
-    pl.semaphore_wait(barrier, blk - 1)
+    pl.semaphore_wait(barrier, 4)
+
+    def halo_part(n, k, src, dst, part, size):
+        at = pl.ds(part * size, size)
+        return remote(src.at[at], dst.at[at], hs_sem.at[n, part], hr_sem.at[n, part], k)
+
     halo = [
-        remote(send_pair, halo_l, hs_sem.at[0], hr_sem.at[0], 1),
-        remote(send_pair, halo_r, hs_sem.at[1], hr_sem.at[1], -1),
-        remote(send_hi, halo_ll, hs_sem.at[2], hr_sem.at[2], 2),
-        remote(send_lo, halo_rr, hs_sem.at[3], hr_sem.at[3], -2),
+        [
+            halo_part(2, 2, send_hi, halo_ll, part, 4),
+            halo_part(3, -2, send_lo, halo_rr, part, 4),
+            halo_part(0, 1, send_pair, halo_l, part, 8),
+            halo_part(1, -1, send_pair, halo_r, part, 8),
+        ]
+        for part in range(2)
     ]
-    for copy in halo:
-        copy.start()
+    for part in halo:
+        for copy in part:
+            copy.start()
+    for k in (2, -2):
+        signal(near_sem, k)
+    for copy in loads[1:10]:
+        copy.wait()
 
     has_l = jnp.where(me > 0, 1.0, 0.0).astype(f32)
     has_ll = jnp.where(me > 1, 1.0, 0.0).astype(f32)
@@ -119,7 +149,10 @@
     lift = lift_ref[...]
     pick = (lax.broadcasted_iota(jnp.int32, (8, 64), 1) % 8
             == lax.broadcasted_iota(jnp.int32, (8, 64), 0))
-    tiled = dot(lift, jnp.where(pick, 1.0, 0.0).astype(bf16))
+    pick = jnp.where(pick, 1.0, 0.0).astype(bf16)
+    tiled = lax.dot_general(
+        lift, pick, (((0,), (0,)), ((), ())), preferred_element_type=f32
+    )
     col_month = lax.broadcasted_iota(jnp.int32, (64, 64), 1) // 8
     placed = [jnp.where(col_month == i, tiled, 0.0) for i in range(8)]
     placed_b = [x.astype(bf16) for x in placed]
@@ -201,9 +234,6 @@
     lane = lax.broadcasted_iota(jnp.int32, (128, 128), 1)
     first, last = lane == 0, lane == 127
 
-    for copy in halo:
-        copy.wait_recv()
-
     def month_step(q, carry):
         highs, lows = [], []
         for i in range(2):
@@ -233,7 +263,14 @@
                 h2s[2 * q + i + 1, :, 128 * m:128 * m + 128] = nxt_h[:, 128 * i:128 * i + 128]
         return carry
 
-    lax.fori_loop(0, 8, month_step, 0)
+    pl.semaphore_wait(near_sem, 2)
+    for k in (4, -4):
+        signal(far_sem, k)
+    for part in range(2):
+        for copy in halo[part]:
+            copy.wait_recv()
+        lax.fori_loop(4 * part, 4 * part + 4, month_step, 0, unroll=4)
+    loads[10].wait()
 
     def window(ref, q):
         return ref[pl.ds(2 * q, 4)].reshape(256, 256)
@@ -248,7 +285,7 @@
         h3s[pl.ds(2 * q + 1, 2)] = (pair(h2s, q, 1).astype(f32) + gel).astype(bf16).reshape(2, 64, 256)
         return carry
 
-    lax.fori_loop(0, 8, grid_step, 0)
+    lax.fori_loop(0, 8, grid_step, 0, unroll=8)
 
     def top_step(q, total):
         inner = lon_sum(dot(wf4[...], window(h3s, q)), first, last)
@@ -280,9 +317,10 @@
         s4s[pl.ds(2 * q + 1, 2)] = (adj * der).astype(bf16).reshape(2, 64, 256)
         return total
 
-    total = lax.fori_loop(0, 8, top_step, within)
+    total = lax.fori_loop(0, 8, top_step, within, unroll=8)
 
     psend[...] = total
+    pl.semaphore_wait(far_sem, 2)
     sums = [
         remote(psend, pbuf.at[k], ps_sem.at[k], pr_sem.at[k], k) for k in range(1, blk)
     ]
@@ -295,7 +333,7 @@
         s3s[pl.ds(2 * q + 1, 2)] = (adj * g3[q]).astype(bf16).reshape(2, 64, 256)
         return carry
 
-    lax.fori_loop(0, 8, back_step, 0)
+    lax.fori_loop(0, 8, back_step, 0, unroll=8)
 
     def low_step(q, carry):
         adj2 = a3[q] + lon_sum(dot(wb3[...], window(s3s, q)), first, last)
@@ -325,15 +363,23 @@
         gs_rr[q] = rows(part[56:64, 0:128], part[56:64, 128:256]).astype(bf16)
         return carry
 
-    lax.fori_loop(0, 8, low_step, 0)
+    def back_part(n, k, src, dst, part, size):
+        at = pl.ds(part * size, size)
+        return remote(src.at[at], dst.at[at], gs_sem.at[n, part], gr_sem.at[n, part], k)
+
     back = [
-        remote(gs_r, gr_l, gs_sem.at[0], gr_sem.at[0], 1),
-        remote(gs_l, gr_r, gs_sem.at[1], gr_sem.at[1], -1),
-        remote(gs_rr, gr_ll, gs_sem.at[2], gr_sem.at[2], 2),
-        remote(gs_ll, gr_rr, gs_sem.at[3], gr_sem.at[3], -2),
+        [
+            back_part(2, 2, gs_rr, gr_ll, part, 2),
+            back_part(3, -2, gs_ll, gr_rr, part, 2),
+            back_part(0, 1, gs_r, gr_l, part, 4),
+            back_part(1, -1, gs_l, gr_r, part, 4),
+        ]
+        for part in range(4)
     ]
-    for copy in back:
-        copy.start()
+    for part in range(4):
+        lax.fori_loop(2 * part, 2 * part + 2, low_step, 0, unroll=2)
+        for copy in back[part]:
+            copy.start()
 
     for copy in sums:
         copy.wait_recv()
@@ -341,12 +387,13 @@
     for k in range(1, blk):
         tile = tile + pbuf[k]
     full = jnp.sum(jnp.sum(tile, axis=1, keepdims=True), axis=0, keepdims=True)
-    norm = jnp.sqrt(full / 4096.0 + 1e-05)
+    norm = jnp.sqrt(full / month_ref.size + 1e-05)
     scale = jnp.broadcast_to(step_size / norm, (8, 128))
 
-    for copy in back:
-        copy.wait_recv()
     for q in range(8):
+        if q % 2 == 0:
+            for copy in back[q // 2]:
+                copy.wait_recv()
         far_l = gr_ll[q].astype(f32) * has_ll
         far_r = gr_rr[q].astype(f32) * has_rr
         for i in range(2):
@@ -357,7 +404,7 @@
                 g = grad[m, l] + near[8 * m:8 * m + 8] + far[m]
                 out_ref[m, l] = base[m, l] - scale * g
 
-    for copy in halo + sums + back:
+    for copy in sum(halo + back, sums):
         copy.wait_send()
 
 
@@ -372,6 +419,11 @@
     vmem = pltpu.VMEM
     dma = pltpu.SemaphoreType.DMA
     scratch = [
+        vmem(sample.shape, f32), vmem(sample.shape, f32),
+        vmem((32, 128), jnp.int32), vmem((32, 128), jnp.int32), vmem((32, 128), jnp.int32),
+        vmem((32, 128), f32), vmem((32, 128), f32),
+        vmem((8, 64), bf16), vmem(month_kernels.shape, bf16), vmem(grid_kernels.shape, bf16),
+        vmem((8, 64), bf16),
         vmem((16, 16, 128), bf16), vmem((8, 16, 128), bf16), vmem((8, 16, 128), bf16),
         vmem((16, 16, 128), bf16), vmem((16, 16, 128), bf16),
         vmem((8, 16, 128), bf16), vmem((8, 16, 128), bf16),
@@ -391,19 +443,20 @@
         vmem((16, 16, 128), bf16), vmem((16, 16, 128), bf16),
         vmem((8, 16, 128), bf16), vmem((8, 16, 128), bf16),
         vmem((8, 128), f32), vmem((blk, 8, 128), f32),
-        dma((4,)), dma((4,)), dma((4,)), dma((4,)), dma((blk,)), dma((blk,)),
+        dma((4, 2)), dma((4, 2)), dma((4, 4)), dma((4, 4)), dma((blk,)), dma((blk,)), dma((11,)),
+        pltpu.SemaphoreType.REGULAR, pltpu.SemaphoreType.REGULAR,
     ]
     return pl.pallas_call(
         functools.partial(kernel, blk),
         out_shape=jax.ShapeDtypeStruct(sample.shape, f32),
-        in_specs=[pl.BlockSpec(memory_space=pltpu.VMEM)] * 11,
+        in_specs=[pl.BlockSpec(memory_space=pl.ANY)] * 11,
         out_specs=pl.BlockSpec(memory_space=pltpu.VMEM),
         scratch_shapes=scratch,
         compiler_params=pltpu.CompilerParams(collective_id=0, has_side_effects=True),
         name="guided_step",
     )(
         sample, fresh_noise, grid(proxy_month), grid(proxy_cell), grid(proxy_var),
-        grid(observed), grid(proxy_weight), lift_weight, month_kernels, grid_kernels, read_weight,
+        grid(observed), grid(proxy_weight), lift_weight.T, month_kernels, grid_kernels, read_weight,
     )
 
 

time: 45 us -> 30.9 us (0.69)
  Pallas kernels: 41.9 us -> 29.3 us
  local copies, waits for them, and re-layouts: 2.95 us -> 1.57 us
    pallas_call x1, Pallas kernels: 41.9 us -> 29.3 us  [shards(): pl.pallas_call(functools.partial(kernel, blk), out_shape=jax.ShapeDtypeSt...]
    unnamed x4 -> x1, local copies, waits for them, and re-layouts: 2.95 us -> 1.57 us
where the time goes in v2:
time: 30.9 us; the launch traced here: 30.8 us
  Pallas kernels  29.3 us (95%)
  local copies, waits for them, and re-layouts  1.57 us (5%)
    pallas_call x1, Pallas kernels, shards(): pl.pallas_call(functools.partial(kernel, blk), out_shape=jax.ShapeDtypeSt...  29.3 us
    unnamed x1, local copies, waits for them, and re-layouts  1.57 us

profile of v2, /device:TPU:16, one launch (start us, length us, event | category | flops | bytes accessed | tf_op | source)
XLA Modules:
  0.0 30.8 jit_solution(6933783127084724993)
XLA Ops:
  0.0 29.3 %guided_step.1 = f32[2,16,8,128]{3,2,1,0:T(8,128)} custom-call(f32[2,16,8,128]{3,2,1,0:T(8,128)} %sample_in.1, f32[2,16,8,128]{3,2,1,0:T(8,128)} %noise_in.1, s32[32,128]{1,0:T(8,128)} %bitcast.6, s32[32,128]{1,0:T(8,128)} %bitcast.7, s32[32,128]{1,0:T(8,128)} %bitcast.8, f32[32,128]{1,0:T(8,128)} %bitcast.9, f32[32,128]{1,0:T(8,128)} %bitcast.10, ...), custom_call_target="tpu_custom_call" | custom-call | tf_op jit(solution)/shard_map/guided_step/pallas_call | solution.py:449
  29.3 1.6 %copy.13 = f32[2,16,8,128]{3,2,1,0:T(8,128)} copy(f32[2,16,8,128]{3,2,1,0:T(8,128)} %guided_step.1) | data formatting | bytes 262144

commit v3 on v2

--- a/solution.py
+++ b/solution.py
@@ -45,25 +45,14 @@
     return jnp.concatenate(parts, axis=0)
 
 
-def lon_sum(out, first, last):
-    halves = []
-    for m in range(2):
-        cols = slice(128 * m, 128 * (m + 1))
-        left = pltpu.roll(out[0:128, cols], 1, 1)
-        right = pltpu.roll(out[256:384, cols], 127, 1)
-        total = out[128:256, cols] + jnp.where(first, 0.0, left) + jnp.where(last, 0.0, right)
-        halves.append(total)
-    return lanes(*halves)
-
-
 def grid_weights(block):
     zero = jnp.zeros((64, 64), f32)
-    out = []
+    upper, lower = [], []
     for b in range(3):
-        k0, k1, k2 = block(0, b), block(1, b), block(2, b)
-        out.append(lanes(k0, k1, k2, zero))
-        out.append(lanes(zero, k0, k1, k2))
-    return rows(*out).astype(bf16)
+        taps = [block(a, b) for a in range(3)]
+        upper += taps + [zero]
+        lower += [zero] + taps
+    return rows(lanes(*upper), lanes(*lower)).astype(bf16)
 
 
 def kernel(
@@ -76,7 +65,7 @@
     send_pair, send_lo, send_hi, halo_l, halo_r, halo_ll, halo_rr,
     wf1, wf2, wf3, wf4, wb4, wb3, wb2, wb1, wread, wreadt,
     field,
-    g1, g2, g3, g4, h2s, h3s, s4s, s3s, a4, a3,
+    h1s, h4s, a1s, g1, g2, g3, g4, h2s, h3s, s4s, s3s, a4, a3,
     base, grad,
     gs_l, gs_r, gs_ll, gs_rr, gr_l, gr_r, gr_ll, gr_rr,
     psend, pbuf,
@@ -126,12 +115,12 @@
 
     halo = [
         [
-            halo_part(2, 2, send_hi, halo_ll, part, 4),
-            halo_part(3, -2, send_lo, halo_rr, part, 4),
-            halo_part(0, 1, send_pair, halo_l, part, 8),
-            halo_part(1, -1, send_pair, halo_r, part, 8),
+            halo_part(2, 2, send_hi, halo_ll, part, 2),
+            halo_part(3, -2, send_lo, halo_rr, part, 2),
+            halo_part(0, 1, send_pair, halo_l, part, 4),
+            halo_part(1, -1, send_pair, halo_r, part, 4),
         ]
-        for part in range(2)
+        for part in range(4)
     ]
     for part in halo:
         for copy in part:
@@ -162,7 +151,7 @@
         acc = acc + dot(mk_ref[0, 1], placed_b[j + 1])
         acc = acc + dot(mk_ref[0, 2], placed_b[j + 2])
         inner_rows.append(acc)
-    both = rows(*inner_rows, *placed[1:7])
+    both = rows(*[x for j in range(6) for x in (inner_rows[j], placed[j + 1])])
     both_hi = both.astype(bf16).astype(f32)
     both_lo = both - both_hi
     wf1[...] = lanes(both_hi, both_lo, both_hi, jnp.zeros_like(both)).astype(bf16)
@@ -228,11 +217,30 @@
 
     zero_row = jnp.zeros((64, 256), bf16)
     for ref in (h2s, h3s, s4s, s3s):
-        ref[0] = zero_row
-        ref[17] = zero_row
+        for tap in range(3):
+            ref[tap, 0] = zero_row
+            ref[tap, 17] = zero_row
 
     lane = lax.broadcasted_iota(jnp.int32, (128, 128), 1)
     first, last = lane == 0, lane == 127
+    zero_half = jnp.zeros((128, 128), bf16)
+
+    def window(ref, q):
+        return rows(*[ref[tap, pl.ds(2 * q, 4)].reshape(256, 256) for tap in range(3)])
+
+    def pair(ref, q):
+        return ref[1, pl.ds(2 * q + 1, 2)].reshape(128, 256)
+
+    def put(ref, q, value):
+        left, right = [], []
+        for m in range(2):
+            half = value[:, 128 * m:128 * m + 128]
+            left.append(jnp.where(first, zero_half, pltpu.roll(half, 1, 1)))
+            right.append(jnp.where(last, zero_half, pltpu.roll(half, 127, 1)))
+        at = pl.ds(2 * q + 1, 2)
+        ref[0, at] = lanes(*left).reshape(2, 64, 256)
+        ref[1, at] = value.reshape(2, 64, 256)
+        ref[2, at] = lanes(*right).reshape(2, 64, 256)
 
     def month_step(q, carry):
         highs, lows = [], []
@@ -249,49 +257,56 @@
             lows.append(rows(z, own - own_hi, z))
         high = lanes(*highs)
         src = rows(high, high, lanes(*lows), jnp.zeros((64, 256), f32)).astype(bf16)
-        out = dot(wf1[...], src)
-        gel, der = gelu_parts(out[0:384])
-        g1[q] = der
-        hidden = out[384:768] + gel
-        hidden_b = hidden.astype(bf16)
+        out = dot(wf1[...], src).astype(bf16)
+        hidden = []
+        for j in range(6):
+            gel, der = gelu_parts(out[128 * j:128 * j + 64])
+            g1[q, 64 * j:64 * j + 64] = der
+            hidden.append(out[128 * j + 64:128 * j + 128] + gel)
+        h1s[q] = rows(*hidden)
+        return carry
+
+    def month_step2(q, carry):
+        halves = []
         for m in range(2):
-            src2 = rows(*[hidden_b[64 * j:64 * j + 64] for j in (m, m + 2, m + 4)])
-            gel2, der2 = gelu_parts(dot(wf2[...], src2))
+            src2 = rows(*[h1s[q, 64 * j:64 * j + 64] for j in (m, m + 2, m + 4)])
+            gel2, der2 = gelu_parts(dot(wf2[...], src2).astype(bf16))
             g2[q, m] = der2
-            nxt_h = (hidden[64 * (m + 2):64 * (m + 3)] + gel2).astype(bf16)
-            for i in range(2):
-                h2s[2 * q + i + 1, :, 128 * m:128 * m + 128] = nxt_h[:, 128 * i:128 * i + 128]
+            nxt_h = h1s[q, 64 * (m + 2):64 * (m + 3)] + gel2
+            halves.append(rows(nxt_h[:, 0:128], nxt_h[:, 128:256]))
+        put(h2s, q, lanes(*halves))
         return carry
 
     pl.semaphore_wait(near_sem, 2)
     for k in (4, -4):
         signal(far_sem, k)
-    for part in range(2):
+    for part in range(4):
         for copy in halo[part]:
             copy.wait_recv()
-        lax.fori_loop(4 * part, 4 * part + 4, month_step, 0, unroll=4)
+        lax.fori_loop(2 * part, 2 * part + 2, month_step, 0, unroll=2)
+    lax.fori_loop(0, 8, month_step2, 0, unroll=8)
     loads[10].wait()
 
-    def window(ref, q):
-        return ref[pl.ds(2 * q, 4)].reshape(256, 256)
-
-    def pair(ref, q, at):
-        return ref[pl.ds(2 * q + at, 2)].reshape(128, 256)
-
     def grid_step(q, carry):
-        inner = lon_sum(dot(wf3[...], window(h2s, q)), first, last)
+        inner = dot(wf3[...], window(h2s, q))
         gel, der = gelu_parts(inner)
-        g3[q] = der
-        h3s[pl.ds(2 * q + 1, 2)] = (pair(h2s, q, 1).astype(f32) + gel).astype(bf16).reshape(2, 64, 256)
+        g3[q] = der.astype(bf16)
+        put(h3s, q, (pair(h2s, q).astype(f32) + gel).astype(bf16))
         return carry
 
     lax.fori_loop(0, 8, grid_step, 0, unroll=8)
 
+    def last_step(q, carry):
+        inner = dot(wf4[...], window(h3s, q))
+        gel, der = gelu_parts(inner)
+        g4[q] = der.astype(bf16)
+        h4s[q] = (pair(h3s, q).astype(f32) + gel).astype(bf16)
+        return carry
+
+    lax.fori_loop(0, 8, last_step, 0, unroll=8)
+
     def top_step(q, total):
-        inner = lon_sum(dot(wf4[...], window(h3s, q)), first, last)
-        gel, der = gelu_parts(inner)
-        hidden = (pair(h3s, q, 1).astype(f32) + gel).astype(bf16)
-        score = dot(wread[...], hidden)
+        score = dot(wread[...], h4s[q])
         forces = []
         for i in range(2):
             l = 2 * q + i
@@ -314,7 +329,7 @@
         src = rows(force_hi, force - force_hi).astype(bf16)
         adj = dot(wreadt[...], src)
         a4[q] = adj
-        s4s[pl.ds(2 * q + 1, 2)] = (adj * der).astype(bf16).reshape(2, 64, 256)
+        put(s4s, q, adj.astype(bf16) * g4[q])
         return total
 
     total = lax.fori_loop(0, 8, top_step, within, unroll=8)
@@ -328,29 +343,38 @@
         copy.start()
 
     def back_step(q, carry):
-        adj = a4[q] + lon_sum(dot(wb4[...], window(s4s, q)), first, last)
+        adj = a4[q] + dot(wb4[...], window(s4s, q))
         a3[q] = adj
-        s3s[pl.ds(2 * q + 1, 2)] = (adj * g3[q]).astype(bf16).reshape(2, 64, 256)
+        put(s3s, q, adj.astype(bf16) * g3[q])
         return carry
 
     lax.fori_loop(0, 8, back_step, 0, unroll=8)
 
     def low_step(q, carry):
-        adj2 = a3[q] + lon_sum(dot(wb3[...], window(s3s, q)), first, last)
+        adj2 = a3[q] + dot(wb3[...], window(s3s, q))
         own, pushed = [], []
         for m in range(2):
             cols = slice(128 * m, 128 * m + 128)
             adj = lanes(adj2[0:64, cols], adj2[64:128, cols])
             own.append(adj)
-            scaled = (adj * g2[q, m]).astype(bf16)
+            scaled = adj.astype(bf16) * g2[q, m]
             pushed.append(dot(wb2[...], scaled))
-        adj1 = rows(
+        adj1 = [
             pushed[0][0:64], pushed[1][0:64],
             own[0] + pushed[0][64:128], own[1] + pushed[1][64:128],
             pushed[0][128:192], pushed[1][128:192],
-        )
-        scaled1 = (adj1 * g1[q]).astype(bf16)
-        both = dot(wb1[...], rows(scaled1, adj1.astype(bf16)))
+        ]
+        src = []
+        for j in range(6):
+            adj = adj1[j].astype(bf16)
+            src += [adj * g1[q, 64 * j:64 * j + 64], adj]
+        a1s[q] = rows(*src)
+        return carry
+
+    lax.fori_loop(0, 8, low_step, 0, unroll=8)
+
+    def lift_step(q, carry):
+        both = dot(wb1[...], a1s[q])
         part = both[0:64] + both[64:128]
         for i in range(2):
             l = 2 * q + i
@@ -377,7 +401,7 @@
         for part in range(4)
     ]
     for part in range(4):
-        lax.fori_loop(2 * part, 2 * part + 2, low_step, 0, unroll=2)
+        lax.fori_loop(2 * part, 2 * part + 2, lift_step, 0, unroll=2)
         for copy in back[part]:
             copy.start()
 
@@ -428,14 +452,15 @@
         vmem((16, 16, 128), bf16), vmem((16, 16, 128), bf16),
         vmem((8, 16, 128), bf16), vmem((8, 16, 128), bf16),
         vmem((768, 256), bf16), vmem((64, 192), bf16),
-        vmem((384, 256), bf16), vmem((384, 256), bf16), vmem((384, 256), bf16), vmem((384, 256), bf16),
+        vmem((128, 768), bf16), vmem((128, 768), bf16), vmem((128, 768), bf16), vmem((128, 768), bf16),
         vmem((192, 64), bf16), vmem((128, 768), bf16),
         vmem((16, 128), bf16), vmem((128, 32), bf16),
         vmem((256, 512), f32),
-        vmem((8, 384, 256), f32), vmem((8, 2, 64, 256), f32),
-        vmem((8, 128, 256), f32), vmem((8, 128, 256), f32),
-        vmem((18, 64, 256), bf16), vmem((18, 64, 256), bf16),
-        vmem((18, 64, 256), bf16), vmem((18, 64, 256), bf16),
+        vmem((8, 384, 256), bf16), vmem((8, 128, 256), bf16), vmem((8, 768, 256), bf16),
+        vmem((8, 384, 256), bf16), vmem((8, 2, 64, 256), bf16), vmem((8, 128, 256), bf16),
+        vmem((8, 128, 256), bf16),
+        vmem((3, 18, 64, 256), bf16), vmem((3, 18, 64, 256), bf16),
+        vmem((3, 18, 64, 256), bf16), vmem((3, 18, 64, 256), bf16),
         vmem((8, 128, 256), f32), vmem((8, 128, 256), f32),
         vmem((2, 16, 8, 128), f32), vmem((2, 16, 8, 128), f32),
         vmem((16, 16, 128), bf16), vmem((16, 16, 128), bf16),
@@ -443,7 +468,7 @@
         vmem((16, 16, 128), bf16), vmem((16, 16, 128), bf16),
         vmem((8, 16, 128), bf16), vmem((8, 16, 128), bf16),
         vmem((8, 128), f32), vmem((blk, 8, 128), f32),
-        dma((4, 2)), dma((4, 2)), dma((4, 4)), dma((4, 4)), dma((blk,)), dma((blk,)), dma((11,)),
+        dma((4, 4)), dma((4, 4)), dma((4, 4)), dma((4, 4)), dma((blk,)), dma((blk,)), dma((11,)),
         pltpu.SemaphoreType.REGULAR, pltpu.SemaphoreType.REGULAR,
     ]
     return pl.pallas_call(
@@ -452,12 +477,12 @@
         in_specs=[pl.BlockSpec(memory_space=pl.ANY)] * 11,
         out_specs=pl.BlockSpec(memory_space=pltpu.VMEM),
         scratch_shapes=scratch,
-        compiler_params=pltpu.CompilerParams(collective_id=0, has_side_effects=True),
+        compiler_params=pltpu.CompilerParams(collective_id=0, has_side_effects=True, vmem_limit_bytes=32 * 1024 * 1024),
         name="guided_step",
-    )(
+    )(*[pltpu.with_memory_space_constraint(x, pltpu.HBM) for x in (
         sample, fresh_noise, grid(proxy_month), grid(proxy_cell), grid(proxy_var),
         grid(observed), grid(proxy_weight), lift_weight.T, month_kernels, grid_kernels, read_weight,
-    )
+    )])
 
 
 def solution(mesh):

time: 30.9 us -> 24.7 us (0.80)
  Pallas kernels: 29.3 us -> 24 us
  local copies, waits for them, and re-layouts: 1.57 us -> 0.66 us
    pallas_call x1, Pallas kernels: 29.3 us -> 24 us  [shards(): pl.pallas_call(functools.partial(kernel, blk), out_shape=jax.ShapeDtypeSt...]
    unnamed x1, local copies, waits for them, and re-layouts: 1.57 us -> 0.66 us
where the time goes in v3:
time: 24.7 us; the launch traced here: 24.6 us
  Pallas kernels  24 us (97%)
  local copies, waits for them, and re-layouts  0.66 us (3%)
    pallas_call x1, Pallas kernels, shards(): pl.pallas_call(functools.partial(kernel, blk), out_shape=jax.ShapeDtypeSt...  24 us
    unnamed x1, local copies, waits for them, and re-layouts  0.66 us

profile of v3, /device:TPU:16, one launch (start us, length us, event | category | flops | bytes accessed | tf_op | source)
XLA Modules:
  0.0 24.6 jit_solution(14004856089788203667)
XLA Ops:
  0.0 24.0 %guided_step.1 = f32[2,16,8,128]{3,2,1,0:T(8,128)S(1)} custom-call(f32[2,16,8,128]{3,2,1,0:T(8,128)} %sample_in.1, f32[2,16,8,128]{3,2,1,0:T(8,128)} %noise_in.1, s32[32,128]{1,0:T(8,128)} %bitcast.6, s32[32,128]{1,0:T(8,128)} %bitcast.7, s32[32,128]{1,0:T(8,128)} %bitcast.8, f32[32,128]{1,0:T(8,128)} %bitcast.9, f32[32,128]{1,0:T(8,128)} %bitcast.10, ...), custom_call_target="tpu_custom_call" | custom-call | tf_op jit(solution)/shard_map/guided_step/pallas_call | solution.py:474
  24.0 0.7 %copy.13 = f32[2,16,8,128]{3,2,1,0:T(8,128)} copy(f32[2,16,8,128]{3,2,1,0:T(8,128)S(1)} %guided_step.1) | data formatting | bytes 262144

commit v4 on v3

--- a/solution.py
+++ b/solution.py
@@ -53,6 +53,28 @@
         upper += taps + [zero]
         lower += [zero] + taps
     return rows(lanes(*upper), lanes(*lower)).astype(bf16)
+
+
+def grid_weights_tall(block):
+    zero = jnp.zeros((64, 64), f32)
+    taps = []
+    for b in range(3):
+        k = [block(a, b) for a in range(3)]
+        taps.append(rows(lanes(*k, zero), lanes(zero, *k)))
+    return rows(*[taps[b][16 * g:16 * g + 16] for g in range(8) for b in range(3)]).astype(bf16)
+
+
+def lon_sum(out, first, last):
+    groups = []
+    for g in range(8):
+        halves = []
+        for m in range(2):
+            tap = [out[48 * g + 16 * b:48 * g + 16 * b + 16, 128 * m:128 * m + 128] for b in range(3)]
+            left = jnp.where(first, 0.0, pltpu.roll(tap[0], 1, 1))
+            right = jnp.where(last, 0.0, pltpu.roll(tap[2], 127, 1))
+            halves.append(tap[1] + left + right)
+        groups.append(lanes(*halves))
+    return rows(*groups)
 
 
 def kernel(
@@ -65,7 +87,7 @@
     send_pair, send_lo, send_hi, halo_l, halo_r, halo_ll, halo_rr,
     wf1, wf2, wf3, wf4, wb4, wb3, wb2, wb1, wread, wreadt,
     field,
-    h1s, h4s, a1s, g1, g2, g3, g4, h2s, h3s, s4s, s3s, a4, a3,
+    f4s, h1s, h4s, a1s, g1, g2, g3, g4, h2s, h3s, s4s, s3s, a4, a3,
     base, grad,
     gs_l, gs_r, gs_ll, gs_rr, gr_l, gr_r, gr_ll, gr_rr,
     psend, pbuf,
@@ -168,8 +190,8 @@
     ).astype(bf16)
     wf3[...] = grid_weights(lambda a, b: gk_ref[0, a, b].astype(f32))
     wf4[...] = grid_weights(lambda a, b: gk_ref[1, a, b].astype(f32))
-    wb3[...] = grid_weights(lambda a, b: jnp.transpose(gk_ref[0, 2 - a, 2 - b].astype(f32)))
-    wb4[...] = grid_weights(lambda a, b: jnp.transpose(gk_ref[1, 2 - a, 2 - b].astype(f32)))
+    wb3[...] = grid_weights_tall(lambda a, b: jnp.transpose(gk_ref[0, 2 - a, 2 - b].astype(f32)))
+    wb4[...] = grid_weights_tall(lambda a, b: jnp.transpose(gk_ref[1, 2 - a, 2 - b].astype(f32)))
     read = read_ref[...].astype(f32)
     zero_read = jnp.zeros((8, 64), f32)
     wide = rows(lanes(read, zero_read), lanes(zero_read, read))
@@ -216,17 +238,25 @@
         within = within - taken[8 * r:8 * r + 8]
 
     zero_row = jnp.zeros((64, 256), bf16)
-    for ref in (h2s, h3s, s4s, s3s):
+    for ref in (s4s, s3s):
+        ref[0] = zero_row
+        ref[17] = zero_row
+    for ref in (h2s, h3s):
         for tap in range(3):
             ref[tap, 0] = zero_row
             ref[tap, 17] = zero_row
 
     lane = lax.broadcasted_iota(jnp.int32, (128, 128), 1)
     first, last = lane == 0, lane == 127
+    lane16 = lax.broadcasted_iota(jnp.int32, (16, 128), 1)
+    first16, last16 = lane16 == 0, lane16 == 127
     zero_half = jnp.zeros((128, 128), bf16)
 
     def window(ref, q):
         return rows(*[ref[tap, pl.ds(2 * q, 4)].reshape(256, 256) for tap in range(3)])
+
+    def rows4(ref, q):
+        return ref[pl.ds(2 * q, 4)].reshape(256, 256)
 
     def pair(ref, q):
         return ref[1, pl.ds(2 * q + 1, 2)].reshape(128, 256)
@@ -277,33 +307,22 @@
         put(h2s, q, lanes(*halves))
         return carry
 
-    pl.semaphore_wait(near_sem, 2)
-    for k in (4, -4):
-        signal(far_sem, k)
-    for part in range(4):
-        for copy in halo[part]:
-            copy.wait_recv()
-        lax.fori_loop(2 * part, 2 * part + 2, month_step, 0, unroll=2)
-    lax.fori_loop(0, 8, month_step2, 0, unroll=8)
-    loads[10].wait()
 
     def grid_step(q, carry):
-        inner = dot(wf3[...], window(h2s, q))
+        inner = dot(wf3[...], window(h2s, q)).astype(bf16)
         gel, der = gelu_parts(inner)
-        g3[q] = der.astype(bf16)
-        put(h3s, q, (pair(h2s, q).astype(f32) + gel).astype(bf16))
-        return carry
-
-    lax.fori_loop(0, 8, grid_step, 0, unroll=8)
+        g3[q] = der
+        put(h3s, q, pair(h2s, q) + gel)
+        return carry
+
 
     def last_step(q, carry):
-        inner = dot(wf4[...], window(h3s, q))
+        inner = dot(wf4[...], window(h3s, q)).astype(bf16)
         gel, der = gelu_parts(inner)
-        g4[q] = der.astype(bf16)
-        h4s[q] = (pair(h3s, q).astype(f32) + gel).astype(bf16)
-        return carry
-
-    lax.fori_loop(0, 8, last_step, 0, unroll=8)
+        g4[q] = der
+        h4s[q] = pair(h3s, q) + gel
+        return carry
+
 
     def top_step(q, total):
         score = dot(wread[...], h4s[q])
@@ -326,13 +345,31 @@
             forces.append(lanes(*line))
         force = rows(*forces)
         force_hi = force.astype(bf16).astype(f32)
-        src = rows(force_hi, force - force_hi).astype(bf16)
-        adj = dot(wreadt[...], src)
+        f4s[q] = rows(force_hi, force - force_hi).astype(bf16)
+        return total
+
+    def adjoint_step(q, carry):
+        adj = dot(wreadt[...], f4s[q])
         a4[q] = adj
-        put(s4s, q, adj.astype(bf16) * g4[q])
-        return total
-
-    total = lax.fori_loop(0, 8, top_step, within, unroll=8)
+        s4s[pl.ds(2 * q + 1, 2)] = (adj.astype(bf16) * g4[q]).reshape(2, 64, 256)
+        return carry
+
+    def run(step, part, carry=0):
+        return lax.fori_loop(2 * part, 2 * part + 2, step, carry, unroll=2)
+
+    pl.semaphore_wait(near_sem, 2)
+    for k in (4, -4):
+        signal(far_sem, k)
+    loads[10].wait()
+    total = within
+    for part in range(4):
+        for copy in halo[part]:
+            copy.wait_recv()
+        run(month_step, part)
+    lax.fori_loop(0, 8, month_step2, 0, unroll=8)
+    lax.fori_loop(0, 8, grid_step, 0, unroll=8)
+    lax.fori_loop(0, 8, last_step, 0, unroll=8)
+    total = lax.fori_loop(0, 8, top_step, total, unroll=8)
 
     psend[...] = total
     pl.semaphore_wait(far_sem, 2)
@@ -341,17 +378,17 @@
     ]
     for copy in sums:
         copy.start()
+    lax.fori_loop(0, 8, adjoint_step, 0, unroll=8)
 
     def back_step(q, carry):
-        adj = a4[q] + dot(wb4[...], window(s4s, q))
+        adj = a4[q] + lon_sum(dot(wb4[...], rows4(s4s, q)), first16, last16)
         a3[q] = adj
-        put(s3s, q, adj.astype(bf16) * g3[q])
-        return carry
-
-    lax.fori_loop(0, 8, back_step, 0, unroll=8)
+        s3s[pl.ds(2 * q + 1, 2)] = (adj.astype(bf16) * g3[q]).reshape(2, 64, 256)
+        return carry
+
 
     def low_step(q, carry):
-        adj2 = a3[q] + dot(wb3[...], window(s3s, q))
+        adj2 = a3[q] + lon_sum(dot(wb3[...], rows4(s3s, q)), first16, last16)
         own, pushed = [], []
         for m in range(2):
             cols = slice(128 * m, 128 * m + 128)
@@ -371,7 +408,6 @@
         a1s[q] = rows(*src)
         return carry
 
-    lax.fori_loop(0, 8, low_step, 0, unroll=8)
 
     def lift_step(q, carry):
         both = dot(wb1[...], a1s[q])
@@ -400,10 +436,17 @@
         ]
         for part in range(4)
     ]
-    for part in range(4):
-        lax.fori_loop(2 * part, 2 * part + 2, lift_step, 0, unroll=2)
-        for copy in back[part]:
-            copy.start()
+    for wave in range(6):
+        if wave == 0:
+            run(back_step, 0)
+        if wave + 1 < 4:
+            run(back_step, wave + 1)
+        if 0 <= wave - 1 < 4:
+            run(low_step, wave - 1)
+        if 0 <= wave - 2 < 4:
+            run(lift_step, wave - 2)
+            for copy in back[wave - 2]:
+                copy.start()
 
     for copy in sums:
         copy.wait_recv()
@@ -452,15 +495,16 @@
         vmem((16, 16, 128), bf16), vmem((16, 16, 128), bf16),
         vmem((8, 16, 128), bf16), vmem((8, 16, 128), bf16),
         vmem((768, 256), bf16), vmem((64, 192), bf16),
-        vmem((128, 768), bf16), vmem((128, 768), bf16), vmem((128, 768), bf16), vmem((128, 768), bf16),
+        vmem((128, 768), bf16), vmem((128, 768), bf16), vmem((384, 256), bf16), vmem((384, 256), bf16),
         vmem((192, 64), bf16), vmem((128, 768), bf16),
         vmem((16, 128), bf16), vmem((128, 32), bf16),
         vmem((256, 512), f32),
+        vmem((8, 32, 256), bf16),
         vmem((8, 384, 256), bf16), vmem((8, 128, 256), bf16), vmem((8, 768, 256), bf16),
         vmem((8, 384, 256), bf16), vmem((8, 2, 64, 256), bf16), vmem((8, 128, 256), bf16),
         vmem((8, 128, 256), bf16),
         vmem((3, 18, 64, 256), bf16), vmem((3, 18, 64, 256), bf16),
-        vmem((3, 18, 64, 256), bf16), vmem((3, 18, 64, 256), bf16),
+        vmem((18, 64, 256), bf16), vmem((18, 64, 256), bf16),
         vmem((8, 128, 256), f32), vmem((8, 128, 256), f32),
         vmem((2, 16, 8, 128), f32), vmem((2, 16, 8, 128), f32),
         vmem((16, 16, 128), bf16), vmem((16, 16, 128), bf16),

time: 24.7 us -> 23.5 us (0.951)
  Pallas kernels: 24 us -> 22.8 us
    pallas_call x1, Pallas kernels: 24 us -> 22.8 us  [shards(): pl.pallas_call(functools.partial(kernel, blk), out_shape=jax.ShapeDtypeSt...]
where the time goes in v4:
time: 23.5 us; the launch traced here: 23.4 us
  Pallas kernels  22.8 us (97%)
  local copies, waits for them, and re-layouts  0.66 us (3%)
    pallas_call x1, Pallas kernels, shards(): pl.pallas_call(functools.partial(kernel, blk), out_shape=jax.ShapeDtypeSt...  22.8 us
    unnamed x1, local copies, waits for them, and re-layouts  0.66 us

profile of v4, /device:TPU:16, one launch (start us, length us, event | category | flops | bytes accessed | tf_op | source)
XLA Modules:
  0.0 23.4 jit_solution(15362864982624222621)
XLA Ops:
  0.0 22.8 %guided_step.1 = f32[2,16,8,128]{3,2,1,0:T(8,128)S(1)} custom-call(f32[2,16,8,128]{3,2,1,0:T(8,128)} %sample_in.1, f32[2,16,8,128]{3,2,1,0:T(8,128)} %noise_in.1, s32[32,128]{1,0:T(8,128)} %bitcast.6, s32[32,128]{1,0:T(8,128)} %bitcast.7, s32[32,128]{1,0:T(8,128)} %bitcast.8, f32[32,128]{1,0:T(8,128)} %bitcast.9, f32[32,128]{1,0:T(8,128)} %bitcast.10, ...), custom_call_target="tpu_custom_call" | custom-call | tf_op jit(solution)/shard_map/guided_step/pallas_call | solution.py:518
  22.8 0.7 %copy.13 = f32[2,16,8,128]{3,2,1,0:T(8,128)} copy(f32[2,16,8,128]{3,2,1,0:T(8,128)S(1)} %guided_step.1) | data formatting | bytes 262144

commit v5 on v4

--- a/solution.py
+++ b/solution.py
@@ -91,7 +91,7 @@
     base, grad,
     gs_l, gs_r, gs_ll, gs_rr, gr_l, gr_r, gr_ll, gr_rr,
     psend, pbuf,
-    hs_sem, hr_sem, gs_sem, gr_sem, ps_sem, pr_sem, in_sem, near_sem, far_sem,
+    hs_sem, hr_sem, gs_sem, gr_sem, ps_sem, pr_sem, in_sem, near_sem, far_sem, wide_sem,
 ):
     me = lax.axis_index("blk")
 
@@ -104,8 +104,51 @@
             device_id={"blk": peer(k)}, device_id_type=MESH,
         )
 
+    def there(k):
+        return jnp.logical_and(me + k >= 0, me + k < blk)
+
+    def count(*ks):
+        return sum(jnp.where(there(k), 1, 0) for k in ks)
+
     def signal(sem, k):
-        pl.semaphore_signal(sem, inc=1, device_id={"blk": peer(k)}, device_id_type=MESH)
+        @pl.when(there(k))
+        def _():
+            pl.semaphore_signal(sem, inc=1, device_id={"blk": peer(k)}, device_id_type=MESH)
+
+    class Link:
+        def __init__(self, src, dst, ssem, rsem, k):
+            self.copy, self.k = remote(src, dst, ssem, rsem, k), k
+
+        def start(self):
+            self.copy.start()
+
+        def wait_send(self):
+            self.copy.wait_send()
+
+        def wait_recv(self):
+            self.copy.wait_recv()
+
+    inside = jnp.logical_and(me >= 2, me < blk - 2)
+
+    def each(links, act, way):
+        @pl.when(inside)
+        def _():
+            for link in links:
+                act(link)
+
+        @pl.when(jnp.logical_not(inside))
+        def _():
+            for link in links:
+                pl.when(there(way * link.k))(functools.partial(act, link))
+
+    def start_all(links):
+        each(links, Link.start, 1)
+
+    def sent_all(links):
+        each(links, Link.wait_send, 1)
+
+    def got_all(links):
+        each(links, Link.wait_recv, -1)
 
     barrier = pltpu.get_barrier_semaphore()
     for k in (2, -2, 1, -1):
@@ -129,33 +172,35 @@
         send_lo[q] = rows(sample_ref[0, 2 * q], sample_ref[0, 2 * q + 1]).astype(bf16)
         send_hi[q] = rows(sample_ref[1, 2 * q], sample_ref[1, 2 * q + 1]).astype(bf16)
 
-    pl.semaphore_wait(barrier, 4)
+    pl.semaphore_wait(barrier, count(1, -1, 2, -2))
 
     def halo_part(n, k, src, dst, part, size):
         at = pl.ds(part * size, size)
-        return remote(src.at[at], dst.at[at], hs_sem.at[n, part], hr_sem.at[n, part], k)
+        return Link(src.at[at], dst.at[at], hs_sem.at[n, part], hr_sem.at[n, part], k)
 
     halo = [
         [
-            halo_part(2, 2, send_hi, halo_ll, part, 2),
-            halo_part(3, -2, send_lo, halo_rr, part, 2),
-            halo_part(0, 1, send_pair, halo_l, part, 4),
-            halo_part(1, -1, send_pair, halo_r, part, 4),
+            halo_part(2, 2, send_hi, halo_ll, part, 4),
+            halo_part(3, -2, send_lo, halo_rr, part, 4),
+            halo_part(0, 1, send_pair, halo_l, part, 8),
+            halo_part(1, -1, send_pair, halo_r, part, 8),
         ]
-        for part in range(4)
+        for part in range(2)
     ]
     for part in halo:
-        for copy in part:
-            copy.start()
+        start_all(part)
+    for k, bufs in ((-1, (halo_l, gr_l)), (1, (halo_r, gr_r)), (-2, (halo_ll, gr_ll)), (2, (halo_rr, gr_rr))):
+        @pl.when(jnp.logical_not(there(k)))
+        def _():
+            for ref in bufs:
+                ref[...] = jnp.zeros(ref.shape, bf16)
     for k in (2, -2):
         signal(near_sem, k)
     for copy in loads[1:10]:
         copy.wait()
 
     has_l = jnp.where(me > 0, 1.0, 0.0).astype(f32)
-    has_ll = jnp.where(me > 1, 1.0, 0.0).astype(f32)
     has_r = jnp.where(me < blk - 1, 1.0, 0.0).astype(f32)
-    has_rr = jnp.where(me < blk - 2, 1.0, 0.0).astype(f32)
 
     lift = lift_ref[...]
     pick = (lax.broadcasted_iota(jnp.int32, (8, 64), 1) % 8
@@ -276,10 +321,10 @@
         highs, lows = [], []
         for i in range(2):
             l = 2 * q + i
-            prev = halo_l[l].astype(f32) * has_l
-            nxt = halo_r[l].astype(f32) * has_r
-            prev2 = halo_ll[q].astype(f32)[8 * i:8 * i + 8] * has_ll
-            nxt2 = halo_rr[q].astype(f32)[8 * i:8 * i + 8] * has_rr
+            prev = halo_l[l].astype(f32)
+            nxt = halo_r[l].astype(f32)
+            prev2 = halo_ll[q].astype(f32)[8 * i:8 * i + 8]
+            nxt2 = halo_rr[q].astype(f32)[8 * i:8 * i + 8]
             own = rows(sample_ref[0, l], sample_ref[1, l])
             own_hi = own.astype(bf16).astype(f32)
             highs.append(rows(prev2, prev, own_hi, nxt, nxt2))
@@ -357,22 +402,24 @@
     def run(step, part, carry=0):
         return lax.fori_loop(2 * part, 2 * part + 2, step, carry, unroll=2)
 
-    pl.semaphore_wait(near_sem, 2)
+    pl.semaphore_wait(near_sem, count(2, -2))
     for k in (4, -4):
         signal(far_sem, k)
     loads[10].wait()
     total = within
-    for part in range(4):
-        for copy in halo[part]:
-            copy.wait_recv()
-        run(month_step, part)
+    for part in range(2):
+        got_all(halo[part])
+        lax.fori_loop(4 * part, 4 * part + 4, month_step, 0, unroll=4)
+    pl.semaphore_wait(far_sem, count(4, -4))
+    for k in (8, -8):
+        signal(wide_sem, k)
     lax.fori_loop(0, 8, month_step2, 0, unroll=8)
     lax.fori_loop(0, 8, grid_step, 0, unroll=8)
     lax.fori_loop(0, 8, last_step, 0, unroll=8)
     total = lax.fori_loop(0, 8, top_step, total, unroll=8)
 
-    psend[...] = total
-    pl.semaphore_wait(far_sem, 2)
+    psend[...] = jnp.sum(total, axis=0, keepdims=True)
+    pl.semaphore_wait(wide_sem, count(8, -8))
     sums = [
         remote(psend, pbuf.at[k], ps_sem.at[k], pr_sem.at[k], k) for k in range(1, blk)
     ]
@@ -425,54 +472,55 @@
 
     def back_part(n, k, src, dst, part, size):
         at = pl.ds(part * size, size)
-        return remote(src.at[at], dst.at[at], gs_sem.at[n, part], gr_sem.at[n, part], k)
+        return Link(src.at[at], dst.at[at], gs_sem.at[n, part], gr_sem.at[n, part], k)
 
     back = [
         [
-            back_part(2, 2, gs_rr, gr_ll, part, 2),
-            back_part(3, -2, gs_ll, gr_rr, part, 2),
-            back_part(0, 1, gs_r, gr_l, part, 4),
-            back_part(1, -1, gs_l, gr_r, part, 4),
+            back_part(2, 2, gs_rr, gr_ll, part, 4),
+            back_part(3, -2, gs_ll, gr_rr, part, 4),
+            back_part(0, 1, gs_r, gr_l, part, 8),
+            back_part(1, -1, gs_l, gr_r, part, 8),
         ]
-        for part in range(4)
+        for part in range(2)
     ]
-    for wave in range(6):
-        if wave == 0:
-            run(back_step, 0)
-        if wave + 1 < 4:
-            run(back_step, wave + 1)
-        if 0 <= wave - 1 < 4:
-            run(low_step, wave - 1)
-        if 0 <= wave - 2 < 4:
-            run(lift_step, wave - 2)
-            for copy in back[wave - 2]:
-                copy.start()
-
+    def half(step, part):
+        lax.fori_loop(4 * part, 4 * part + 4, step, 0, unroll=4)
+
+    half(back_step, 0)
+    half(back_step, 1)
+    half(low_step, 0)
+    half(lift_step, 0)
+    start_all(back[0])
+    half(low_step, 1)
+    half(lift_step, 1)
+    start_all(back[1])
+
+    for copy in sums:
+        copy.wait_send()
+    sent_all(halo[0] + halo[1] + back[0])
     for copy in sums:
         copy.wait_recv()
     tile = psend[...]
     for k in range(1, blk):
         tile = tile + pbuf[k]
-    full = jnp.sum(jnp.sum(tile, axis=1, keepdims=True), axis=0, keepdims=True)
+    full = jnp.sum(tile, axis=1, keepdims=True)
     norm = jnp.sqrt(full / month_ref.size + 1e-05)
     scale = jnp.broadcast_to(step_size / norm, (8, 128))
 
     for q in range(8):
-        if q % 2 == 0:
-            for copy in back[q // 2]:
-                copy.wait_recv()
-        far_l = gr_ll[q].astype(f32) * has_ll
-        far_r = gr_rr[q].astype(f32) * has_rr
+        if q % 4 == 0:
+            got_all(back[q // 4])
+        far_l = gr_ll[q].astype(f32)
+        far_r = gr_rr[q].astype(f32)
         for i in range(2):
             l = 2 * q + i
-            near = gr_l[l].astype(f32) * has_l + gr_r[l].astype(f32) * has_r
+            near = gr_l[l].astype(f32) + gr_r[l].astype(f32)
             far = (far_l[8 * i:8 * i + 8], far_r[8 * i:8 * i + 8])
             for m in range(2):
                 g = grad[m, l] + near[8 * m:8 * m + 8] + far[m]
                 out_ref[m, l] = base[m, l] - scale * g
 
-    for copy in sum(halo + back, sums):
-        copy.wait_send()
+    sent_all(back[1])
 
 
 def shards(
@@ -511,9 +559,9 @@
         vmem((8, 16, 128), bf16), vmem((8, 16, 128), bf16),
         vmem((16, 16, 128), bf16), vmem((16, 16, 128), bf16),
         vmem((8, 16, 128), bf16), vmem((8, 16, 128), bf16),
-        vmem((8, 128), f32), vmem((blk, 8, 128), f32),
+        vmem((1, 128), f32), vmem((blk, 1, 128), f32),
         dma((4, 4)), dma((4, 4)), dma((4, 4)), dma((4, 4)), dma((blk,)), dma((blk,)), dma((11,)),
-        pltpu.SemaphoreType.REGULAR, pltpu.SemaphoreType.REGULAR,
+        pltpu.SemaphoreType.REGULAR, pltpu.SemaphoreType.REGULAR, pltpu.SemaphoreType.REGULAR,
     ]
     return pl.pallas_call(
         functools.partial(kernel, blk),

time: 23.5 us -> 23.3 us (level)
  the two profiles are of different devices: /device:TPU:16 before, /device:TPU:6 now
where the time goes in v5:
time: 23.3 us; the launch traced here: 23.2 us
  Pallas kernels  22.5 us (97%)
  local copies, waits for them, and re-layouts  0.66 us (3%)
    pallas_call x1, Pallas kernels, shards(): pl.pallas_call(functools.partial(kernel, blk), out_shape=jax.ShapeDtypeSt...  22.5 us
    unnamed x1, local copies, waits for them, and re-layouts  0.66 us

profile of v5, /device:TPU:6, one launch (start us, length us, event | category | flops | bytes accessed | tf_op | source)
XLA Modules:
  0.0 23.2 jit_solution(777470353401852506)
XLA Ops:
  0.0 22.5 %guided_step.1 = f32[2,16,8,128]{3,2,1,0:T(8,128)S(1)} custom-call(f32[2,16,8,128]{3,2,1,0:T(8,128)} %sample_in.1, f32[2,16,8,128]{3,2,1,0:T(8,128)} %noise_in.1, s32[32,128]{1,0:T(8,128)} %bitcast.6, s32[32,128]{1,0:T(8,128)} %bitcast.7, s32[32,128]{1,0:T(8,128)} %bitcast.8, f32[32,128]{1,0:T(8,128)} %bitcast.9, f32[32,128]{1,0:T(8,128)} %bitcast.10, ...), custom_call_target="tpu_custom_call" | custom-call | tf_op jit(solution)/shard_map/guided_step/pallas_call | solution.py:566
  22.5 0.7 %copy.13 = f32[2,16,8,128]{3,2,1,0:T(8,128)} copy(f32[2,16,8,128]{3,2,1,0:T(8,128)S(1)} %guided_step.1) | data formatting | bytes 262144

commit v6 on v4

--- a/solution.py
+++ b/solution.py
@@ -137,12 +137,12 @@
 
     halo = [
         [
-            halo_part(2, 2, send_hi, halo_ll, part, 2),
-            halo_part(3, -2, send_lo, halo_rr, part, 2),
-            halo_part(0, 1, send_pair, halo_l, part, 4),
-            halo_part(1, -1, send_pair, halo_r, part, 4),
+            halo_part(2, 2, send_hi, halo_ll, part, 4),
+            halo_part(3, -2, send_lo, halo_rr, part, 4),
+            halo_part(0, 1, send_pair, halo_l, part, 8),
+            halo_part(1, -1, send_pair, halo_r, part, 8),
         ]
-        for part in range(4)
+        for part in range(2)
     ]
     for part in halo:
         for copy in part:
@@ -362,16 +362,16 @@
         signal(far_sem, k)
     loads[10].wait()
     total = within
-    for part in range(4):
+    for part in range(2):
         for copy in halo[part]:
             copy.wait_recv()
-        run(month_step, part)
+        lax.fori_loop(4 * part, 4 * part + 4, month_step, 0, unroll=4)
     lax.fori_loop(0, 8, month_step2, 0, unroll=8)
     lax.fori_loop(0, 8, grid_step, 0, unroll=8)
     lax.fori_loop(0, 8, last_step, 0, unroll=8)
     total = lax.fori_loop(0, 8, top_step, total, unroll=8)
 
-    psend[...] = total
+    psend[...] = jnp.sum(total, axis=0, keepdims=True)
     pl.semaphore_wait(far_sem, 2)
     sums = [
         remote(psend, pbuf.at[k], ps_sem.at[k], pr_sem.at[k], k) for k in range(1, blk)
@@ -429,37 +429,41 @@
 
     back = [
         [
-            back_part(2, 2, gs_rr, gr_ll, part, 2),
-            back_part(3, -2, gs_ll, gr_rr, part, 2),
-            back_part(0, 1, gs_r, gr_l, part, 4),
-            back_part(1, -1, gs_l, gr_r, part, 4),
+            back_part(2, 2, gs_rr, gr_ll, part, 4),
+            back_part(3, -2, gs_ll, gr_rr, part, 4),
+            back_part(0, 1, gs_r, gr_l, part, 8),
+            back_part(1, -1, gs_l, gr_r, part, 8),
         ]
-        for part in range(4)
+        for part in range(2)
     ]
-    for wave in range(6):
-        if wave == 0:
-            run(back_step, 0)
-        if wave + 1 < 4:
-            run(back_step, wave + 1)
-        if 0 <= wave - 1 < 4:
-            run(low_step, wave - 1)
-        if 0 <= wave - 2 < 4:
-            run(lift_step, wave - 2)
-            for copy in back[wave - 2]:
-                copy.start()
-
+    def half(step, part):
+        lax.fori_loop(4 * part, 4 * part + 4, step, 0, unroll=4)
+
+    half(back_step, 0)
+    half(back_step, 1)
+    half(low_step, 0)
+    half(lift_step, 0)
+    for copy in back[0]:
+        copy.start()
+    half(low_step, 1)
+    half(lift_step, 1)
+    for copy in back[1]:
+        copy.start()
+
+    for copy in sum(halo, sums) + sum(back[:1], []):
+        copy.wait_send()
     for copy in sums:
         copy.wait_recv()
     tile = psend[...]
     for k in range(1, blk):
         tile = tile + pbuf[k]
-    full = jnp.sum(jnp.sum(tile, axis=1, keepdims=True), axis=0, keepdims=True)
+    full = jnp.sum(tile, axis=1, keepdims=True)
     norm = jnp.sqrt(full / month_ref.size + 1e-05)
     scale = jnp.broadcast_to(step_size / norm, (8, 128))
 
     for q in range(8):
-        if q % 2 == 0:
-            for copy in back[q // 2]:
+        if q % 4 == 0:
+            for copy in back[q // 4]:
                 copy.wait_recv()
         far_l = gr_ll[q].astype(f32) * has_ll
         far_r = gr_rr[q].astype(f32) * has_rr
@@ -471,7 +475,7 @@
                 g = grad[m, l] + near[8 * m:8 * m + 8] + far[m]
                 out_ref[m, l] = base[m, l] - scale * g
 
-    for copy in sum(halo + back, sums):
+    for copy in back[1]:
         copy.wait_send()
 
 
@@ -511,7 +515,7 @@
         vmem((8, 16, 128), bf16), vmem((8, 16, 128), bf16),
         vmem((16, 16, 128), bf16), vmem((16, 16, 128), bf16),
         vmem((8, 16, 128), bf16), vmem((8, 16, 128), bf16),
-        vmem((8, 128), f32), vmem((blk, 8, 128), f32),
+        vmem((1, 128), f32), vmem((blk, 1, 128), f32),
         dma((4, 4)), dma((4, 4)), dma((4, 4)), dma((4, 4)), dma((blk,)), dma((blk,)), dma((11,)),
         pltpu.SemaphoreType.REGULAR, pltpu.SemaphoreType.REGULAR,
     ]

time: 23.5 us -> 23.3 us (level)
  no operation moved by 1% of the time
where the time goes in v6:
time: 23.3 us; the launch traced here: 23.2 us
  Pallas kernels  22.6 us (97%)
  local copies, waits for them, and re-layouts  0.66 us (3%)
    pallas_call x1, Pallas kernels, shards(): pl.pallas_call(functools.partial(kernel, blk), out_shape=jax.ShapeDtypeSt...  22.6 us
    unnamed x1, local copies, waits for them, and re-layouts  0.66 us

profile of v6, /device:TPU:16, one launch (start us, length us, event | category | flops | bytes accessed | tf_op | source)
XLA Modules:
  0.0 23.2 jit_solution(8964157358516007442)
XLA Ops:
  0.0 22.6 %guided_step.1 = f32[2,16,8,128]{3,2,1,0:T(8,128)S(1)} custom-call(f32[2,16,8,128]{3,2,1,0:T(8,128)} %sample_in.1, f32[2,16,8,128]{3,2,1,0:T(8,128)} %noise_in.1, s32[32,128]{1,0:T(8,128)} %bitcast.6, s32[32,128]{1,0:T(8,128)} %bitcast.7, s32[32,128]{1,0:T(8,128)} %bitcast.8, f32[32,128]{1,0:T(8,128)} %bitcast.9, f32[32,128]{1,0:T(8,128)} %bitcast.10, ...), custom_call_target="tpu_custom_call" | custom-call | tf_op jit(solution)/shard_map/guided_step/pallas_call | solution.py:522
  22.6 0.7 %copy.13 = f32[2,16,8,128]{3,2,1,0:T(8,128)} copy(f32[2,16,8,128]{3,2,1,0:T(8,128)S(1)} %guided_step.1) | data formatting | bytes 262144

commit v7 on v5

--- a/solution.py
+++ b/solution.py
@@ -221,7 +221,7 @@
     both = rows(*[x for j in range(6) for x in (inner_rows[j], placed[j + 1])])
     both_hi = both.astype(bf16).astype(f32)
     both_lo = both - both_hi
-    wf1[...] = lanes(both_hi, both_lo, both_hi, jnp.zeros_like(both)).astype(bf16)
+    wf1[...] = lanes(both_hi, both_lo, both_hi).astype(bf16)
     flipped_hi = jnp.transpose(both_hi)
     flipped_lo = jnp.transpose(both_lo)
     wb1[...] = rows(flipped_hi, flipped_lo).astype(bf16)
@@ -331,7 +331,7 @@
             z = jnp.zeros((24, 128), f32)
             lows.append(rows(z, own - own_hi, z))
         high = lanes(*highs)
-        src = rows(high, high, lanes(*lows), jnp.zeros((64, 256), f32)).astype(bf16)
+        src = rows(high, high, lanes(*lows)).astype(bf16)
         out = dot(wf1[...], src).astype(bf16)
         hidden = []
         for j in range(6):
@@ -542,7 +542,7 @@
         vmem((16, 16, 128), bf16), vmem((8, 16, 128), bf16), vmem((8, 16, 128), bf16),
         vmem((16, 16, 128), bf16), vmem((16, 16, 128), bf16),
         vmem((8, 16, 128), bf16), vmem((8, 16, 128), bf16),
-        vmem((768, 256), bf16), vmem((64, 192), bf16),
+        vmem((768, 192), bf16), vmem((64, 192), bf16),
         vmem((128, 768), bf16), vmem((128, 768), bf16), vmem((384, 256), bf16), vmem((384, 256), bf16),
         vmem((192, 64), bf16), vmem((128, 768), bf16),
         vmem((16, 128), bf16), vmem((128, 32), bf16),

time: 23.3 us -> 23.3 us (level)
  the two profiles are of different devices: /device:TPU:6 before, /device:TPU:22 now
where the time goes in v7:
time: 23.3 us; the launch traced here: 23.2 us
  Pallas kernels  22.5 us (97%)
  local copies, waits for them, and re-layouts  0.66 us (3%)
    pallas_call x1, Pallas kernels, shards(): pl.pallas_call(functools.partial(kernel, blk), out_shape=jax.ShapeDtypeSt...  22.5 us
    unnamed x1, local copies, waits for them, and re-layouts  0.66 us

profile of v7, /device:TPU:22, one launch (start us, length us, event | category | flops | bytes accessed | tf_op | source)
XLA Modules:
  0.0 23.2 jit_solution(15099472140527634654)
XLA Ops:
  0.0 22.5 %guided_step.1 = f32[2,16,8,128]{3,2,1,0:T(8,128)S(1)} custom-call(f32[2,16,8,128]{3,2,1,0:T(8,128)} %sample_in.1, f32[2,16,8,128]{3,2,1,0:T(8,128)} %noise_in.1, s32[32,128]{1,0:T(8,128)} %bitcast.6, s32[32,128]{1,0:T(8,128)} %bitcast.7, s32[32,128]{1,0:T(8,128)} %bitcast.8, f32[32,128]{1,0:T(8,128)} %bitcast.9, f32[32,128]{1,0:T(8,128)} %bitcast.10, ...), custom_call_target="tpu_custom_call" | custom-call | tf_op jit(solution)/shard_map/guided_step/pallas_call | solution.py:566
  22.5 0.7 %copy.13 = f32[2,16,8,128]{3,2,1,0:T(8,128)} copy(f32[2,16,8,128]{3,2,1,0:T(8,128)S(1)} %guided_step.1) | data formatting | bytes 262144
